TPU v7x, 128 devices: a whole 4x4x4 slice. The times are simulated.
128 devices in a mesh: dp: 16 (over y, z), ctx: 8 (over x, core).
Axes of the slice: x: 4, y: 4, z: 4, core: 2. Of those that a mesh axis runs over, the one named last changes fastest.
Arguments:
- state_input: bfloat16 [32768, 4096], P(('dp', 'ctx')), may hold values from -6 to 6
- gate_values: bfloat16 [32768, 4096], P(('dp', 'ctx')), may hold values from -6 to 6
- input_matrix: bfloat16 [32768, 512], P(('dp', 'ctx')), may hold values from -1.2 to 1.2
- readout_matrix: bfloat16 [32768, 512], P(('dp', 'ctx')), may hold values from -1.1953125 to 1.1953125
- step_unbiased: float32 [32768, 64], P(('dp', 'ctx')), may hold values from -3 to 2560
- step_bias: float32 [64], replicated, may hold values from -1 to 0.5
- decay_rate_log: float32 [64], replicated
- skip_coefficients: float32 [64], replicated, may hold values from 3 to 10
- norm_gain: float32 [4096], replicated, may hold values from 0.1 to 8
- adapter_down: bfloat16 [64, 4096], replicated, may hold values from -0.09375 to 0.09375
- adapter_up: bfloat16 [64, 2048], replicated, may hold values from -0.75 to 0.75
- projection_weight: bfloat16 [2048, 4096], P(('dp', 'ctx')), may hold values from -0.09375 to 0.09375
- output_cotangent: bfloat16 [32768, 2048], P(('dp', 'ctx')), may hold values from -30 to 30
Outputs:
- input_gradient: bfloat16 [32768, 4096], P(('dp', 'ctx'))
- adapter_down_gradient: float32 [64, 4096], P(None, ('dp', 'ctx'))
- adapter_up_gradient: float32 [64, 2048], P(None, ('dp', 'ctx'))
All inputs are finite; a program needn't handle non-finite values.
Results may differ from a plain program's by a relative error of at most 0.009.
Values may be sent and summed in bfloat16 or wider, within the bound.
A program may use at most 192 MiB of HBM per device.

v0:
```python
import jax
import jax.numpy as jnp
from jax import lax
from jax.sharding import PartitionSpec as P

H = 64
P_SIZE = 64
N = 128
G = 4
Q = 256
INNER_CHANNELS = 4096


EPS_NORM = 1e-05
CLIP_EPSILON = 1e-06
ADAPTER_SCALE = 2.0


def entering(value, axis, join, neutral):
    count, mine = (lax.axis_size(axis), lax.axis_index(axis))
    pieces = jax.tree.map(lambda part: lax.all_gather(part, axis), value)
    running = jax.tree.map(
        lambda part, zero: jnp.full_like(part, 0) + jnp.asarray(zero, part.dtype), value, neutral
    )

    def lap(position, running):
        longer = join(running, jax.tree.map(lambda part: part[position], pieces))
        return jax.tree.map(lambda new, old: jnp.where(position < mine, new, old), longer, running)

    return lax.fori_loop(0, count - 1, lap, running)


def carried_in(value, axis, join, neutral):
    count = lax.axis_size(axis)
    place = lax.axis_index(axis)
    ahead = count - 1 - place
    gathered = jax.tree.map(
        lambda a, kind: lax.all_gather(a.astype(kind), axis), value, (jnp.bfloat16, jnp.bfloat16)
    )
    state = jax.tree.map(lambda a, e: jnp.zeros_like(a) + jnp.asarray(e, a.dtype), value, neutral)

    def one(lap, state):
        source = count - 1 - lap
        return join(
            state,
            jax.tree.map(
                lambda a, own: lax.dynamic_index_in_dim(a, source, 0, False).astype(own.dtype),
                gathered,
                value,
            ),
        )

    return lax.fori_loop(0, ahead, one, state)


def combine(earlier, later):
    return (earlier[0] * later[0], earlier[1] * later[0][:, None, None] + later[1])


def spread_heads(grouped, lead):
    wide = jnp.broadcast_to(grouped[..., :, None, :], lead + (G, H // G, grouped.shape[-1]))
    return wide.reshape(lead + (H, grouped.shape[-1]))


def on_device(
    state_input,
    gate_values,
    input_matrix,
    readout_matrix,
    step_unbiased,
    step_bias,
    decay_rate_log,
    skip_coefficients,
    norm_gain,
    adapter_down,
    adapter_up,
    projection_weight,
    output_cotangent,
):
    row_count = state_input.shape[0]
    block_count = row_count // Q
    group_width = INNER_CHANNELS // G
    per_group = H // G
    step_size = jax.nn.softplus(step_unbiased + step_bias[None, :])
    cum_decay = jnp.cumsum(
        (-jnp.exp(decay_rate_log)[None, :] * step_size).reshape(block_count, Q, H), axis=1
    )
    block_total = cum_decay[:, -1, :]
    x_heads = state_input.reshape(row_count, H, P_SIZE)
    xdt_all = (
        (x_heads * step_size[:, :, None]).astype(jnp.bfloat16).reshape(block_count, Q, H, P_SIZE)
    )
    b_blocks = input_matrix.reshape(block_count, Q, G, N)
    c_blocks = readout_matrix.reshape(block_count, Q, G, N)
    inner_prod = jnp.einsum(
        "kign,kjgn->kgij", c_blocks, b_blocks, preferred_element_type=jnp.float32
    )
    inner_prod = jnp.broadcast_to(
        inner_prod[:, :, None], (block_count, G, per_group, Q, Q)
    ).reshape(block_count, H, Q, Q)
    cum_heads = jnp.swapaxes(cum_decay, 1, 2)
    gap_logs = cum_heads[:, :, :, None] - cum_heads[:, :, None, :]
    causal = (
        lax.broadcasted_iota(jnp.int32, (Q, Q), 0) >= lax.broadcasted_iota(jnp.int32, (Q, Q), 1)
    )[None, None]
    scores = (
        inner_prod * jnp.where(causal, jnp.exp(jnp.where(causal, gap_logs, 0.0)), 0.0)
    ).astype(jnp.bfloat16)
    intra_part = jnp.einsum("khij,kjhp->kihp", scores, xdt_all, preferred_element_type=jnp.float32)
    b_heads = spread_heads(b_blocks, (block_count, Q))
    b_weighted = (jnp.exp(block_total[:, None, :] - cum_decay)[..., None] * b_heads).astype(
        jnp.bfloat16
    )
    block_state = jnp.einsum(
        "kjhn,kjhp->khnp", b_weighted, xdt_all, preferred_element_type=jnp.float32
    )

    def step_forward(run_state, block_item):
        decay_log, fresh_state = block_item
        return (jnp.exp(decay_log)[:, None, None] * run_state + fresh_state, run_state)

    zero_state = jnp.zeros((H, N, P_SIZE), jnp.float32)
    device_state, local_in = lax.scan(step_forward, zero_state, (block_total, block_state))
    device_decay = jnp.exp(jnp.sum(block_total, axis=0))
    identity = (jnp.ones((H,), jnp.float32), zero_state)
    unused_decay, incoming = entering((device_decay, device_state), "ctx", combine, identity)
    before = jnp.cumsum(block_total, axis=0) - block_total
    state_in = local_in + jnp.exp(before)[:, :, None, None] * incoming[None]
    incoming_bf = state_in.astype(jnp.bfloat16).reshape(block_count, G, per_group, N, P_SIZE)
    inter_part = jnp.einsum(
        "kign,kgmnp->kigmp", c_blocks, incoming_bf, preferred_element_type=jnp.float32
    ).reshape(block_count, Q, H, P_SIZE)
    ssd_heads = (intra_part + jnp.exp(cum_decay)[..., None] * inter_part).reshape(
        row_count, H, P_SIZE
    ) + skip_coefficients[None, :, None] * x_heads
    silu_z = jax.nn.silu(gate_values.astype(jnp.float32))
    weight_groups = norm_gain.reshape(G, group_width)
    gated = (ssd_heads.reshape(row_count, INNER_CHANNELS) * silu_z).reshape(
        row_count, G, group_width
    )
    rstd = lax.rsqrt(jnp.mean(gated * gated, axis=-1, keepdims=True) + EPS_NORM)
    normalized = (
        (gated * rstd * weight_groups).reshape(row_count, INNER_CHANNELS).astype(jnp.bfloat16)
    )
    down_product = lax.dot_general(
        normalized, adapter_down, (((1,), (1,)), ((), ())), preferred_element_type=jnp.float32
    ).astype(jnp.bfloat16)
    upper_gradient = lax.dot_general(
        output_cotangent, adapter_up, (((1,), (1,)), ((), ())), preferred_element_type=jnp.float32
    ).astype(jnp.bfloat16)
    down_portion = ADAPTER_SCALE * lax.dot_general(
        upper_gradient, normalized, (((0,), (0,)), ((), ())), preferred_element_type=jnp.float32
    )
    up_portion = ADAPTER_SCALE * lax.dot_general(
        down_product, output_cotangent, (((0,), (0,)), ((), ())), preferred_element_type=jnp.float32
    )
    adapter_initial = ADAPTER_SCALE * jnp.dot(
        upper_gradient, adapter_down, preferred_element_type=jnp.float32
    )
    combined_weight = lax.all_gather(projection_weight, ("dp", "ctx"), axis=0, tiled=True)
    normed_gradient = adapter_initial + jnp.dot(
        output_cotangent, combined_weight, preferred_element_type=jnp.float32
    )
    weighted_grad = normed_gradient.reshape(row_count, G, group_width) * weight_groups
    d_gated = rstd * weighted_grad - gated * (rstd * rstd * rstd) * jnp.mean(
        gated * weighted_grad, axis=-1, keepdims=True
    )
    d_ssd = d_gated.reshape(row_count, INNER_CHANNELS) * silu_z
    d_ssd_bf = d_ssd.reshape(block_count, Q, H, P_SIZE).astype(jnp.bfloat16)
    intra_back = jnp.einsum("khij,kihp->kjhp", scores, d_ssd_bf, preferred_element_type=jnp.float32)
    c_heads = spread_heads(c_blocks, (block_count, Q))
    c_weighted = (jnp.exp(cum_decay)[..., None] * c_heads).astype(jnp.bfloat16)
    block_grad = jnp.einsum(
        "kihn,kihp->khnp", c_weighted, d_ssd_bf, preferred_element_type=jnp.float32
    )

    def step_backward(grad_state, block_item):
        decay_log, fresh_state = block_item
        return (jnp.exp(decay_log)[:, None, None] * grad_state + fresh_state, grad_state)

    device_grad, local_out = lax.scan(
        step_backward, zero_state, (block_total, block_grad), reverse=True
    )
    unused_back, outgoing = carried_in((device_decay, device_grad), "ctx", combine, identity)
    after_sum = jnp.flip(jnp.cumsum(jnp.flip(block_total, axis=0), axis=0), axis=0) - block_total
    grad_in = local_out + jnp.exp(after_sum)[:, :, None, None] * outgoing[None]
    outgoing_bf = grad_in.astype(jnp.bfloat16)
    cross_part = jnp.einsum(
        "kjhn,khnp->kjhp", b_weighted, outgoing_bf, preferred_element_type=jnp.float32
    )
    grad_heads = step_size[:, :, None] * (intra_back + cross_part).reshape(
        row_count, H, P_SIZE
    ) + skip_coefficients[None, :, None] * d_ssd.reshape(row_count, H, P_SIZE)
    input_gradient = grad_heads.reshape(row_count, INNER_CHANNELS).astype(jnp.bfloat16)
    down_total, up_total = lax.psum((down_portion, up_portion), ("dp", "ctx"))
    down_root_mean = jnp.sqrt(jnp.mean(down_total * down_total) + CLIP_EPSILON)
    up_root_mean = jnp.sqrt(jnp.mean(up_total * up_total) + CLIP_EPSILON)
    device_total = lax.axis_size(("dp", "ctx"))
    position = lax.axis_index(("dp", "ctx"))
    width_a = down_total.shape[1] // device_total
    width_b = up_total.shape[1] // device_total
    down_fraction = lax.dynamic_slice_in_dim(down_total, position * width_a, width_a, 1)
    up_fraction = lax.dynamic_slice_in_dim(up_total, position * width_b, width_b, 1)
    adapter_down_gradient = down_fraction / jnp.maximum(1.0, down_root_mean)
    adapter_up_gradient = up_fraction / jnp.maximum(1.0, up_root_mean)
    return (input_gradient, adapter_down_gradient, adapter_up_gradient)


def solution(mesh):
    placed = (
        P(("dp", "ctx"), None),
        P(("dp", "ctx"), None),
        P(("dp", "ctx"), None),
        P(("dp", "ctx"), None),
        P(("dp", "ctx"), None),
        P(),
        P(),
        P(),
        P(),
        P(),
        P(),
        P(("dp", "ctx"), None),
        P(("dp", "ctx"), None),
    )
    return jax.shard_map(
        on_device,
        mesh=mesh,
        in_specs=placed,
        out_specs=(P(("dp", "ctx"), None), P(None, ("dp", "ctx")), P(None, ("dp", "ctx"))),
        check_vma=False,
    )
```

profile of v0, /device:TPU:0, one launch (start us, length us, event | category | flops | bytes accessed | tf_op | source)
XLA Modules:
  0.0 570.3 jit_solution(756266060873161029)
XLA Ops:
  14.8 3.0 copy.131
  17.7 3.8 fusion.3
  28.1 5.6 fusion.1
  33.8 11.3 %all-gather = f32[8,1,64]{2,1,0:T(1,128)} all-gather(f32[1,1,64]{2,1,0:T(1,128)S(1)} %copy-done.22), channel_id=2, replica_groups=mesh['dp'=16,'ctx'=8] {'ctx'}, dimensions={0}, use_global_device_ids=true | all-gather | bytes 2304 | tf_op jit(solution)/shard_map/all_gather | solution.py:21
  46.1 67.2 %all-gather.10.cloned.1.call-done = f32[512,128,64]{1,2,0:T(8,128)} async-done(((f32[64,128,64]{1,2,0:T(8,128)}), f32[512,128,64]{1,2,0:T(8,128)}) %all-gather.10.cloned.1.call-update) | async-done | bytes 16777232 | tf_op jit(solution)/shard_map/all_gather | solution.py:21
  113.3 80.0 %while.19 = (s32[]{:T(128)}, f32[64,128,64]{2,1,0:T(8,128)}, s32[]{:T(128)}, f32[8,64]{1,0:T(8,128)}, f32[8,64,128,64]{2,3,1,0:T(8,128)}, /*index=5*/s32[]{:T(128)}, s32[]{:T(128)}) while((s32[]{:T(128)}, f32[64,128,64]{2,1,0:T(8,128)}, s32[]{:T(128)}, f32[8,64]{1,0:T(8,128)}, f32[8,64,128,64]{2,3,1,0:T(8,128)}, ...), condition=%wide.region_3.4_spmd.clone, body=%wide.region_2.3_spmd.clone.sunk | while | flops 2097156 | bytes 14680945 | solution.py:30
  118.5 4.9 fusion.43
  125.1 2.8 copy.195
  128.6 6.1 %fusion.43 = f32[64,128,64]{2,1,0:T(8,128)} fusion(f32[1,64,128,64]{3,2,1,0:T(8,128)} %copy.195, f32[64,128,64]{2,1,0:T(8,128)} %get-tuple-element.418, f32[64]{0:T(128)S(1)} %dynamic-slice_bitcast_fusion.2, pred[]{:T(512)S(6)} %compare.3, pred[]{:T(512)S(6)} %lt.51), kind=kLoop, calls=%fused_computation.4.clone.1 | loop fusion | flops 2097152 | bytes 6291714 | tf_op jit(solution)/shard_map/while/body/eval_jaxpr/jit(_where)/select_n | solution.py:28
  139.9 6.1 %fusion.43 = f32[64,128,64]{2,1,0:T(8,128)} fusion(f32[1,64,128,64]{3,2,1,0:T(8,128)} %copy.195, f32[64,128,64]{2,1,0:T(8,128)} %get-tuple-element.418, f32[64]{0:T(128)S(1)} %dynamic-slice_bitcast_fusion.2, pred[]{:T(512)S(6)} %compare.3, pred[]{:T(512)S(6)} %lt.51), kind=kLoop, calls=%fused_computation.4.clone.1 | loop fusion | flops 2097152 | bytes 6291714 | tf_op jit(solution)/shard_map/while/body/eval_jaxpr/jit(_where)/select_n | solution.py:28
  151.2 6.3 %fusion.43 = f32[64,128,64]{2,1,0:T(8,128)} fusion(f32[1,64,128,64]{3,2,1,0:T(8,128)} %copy.195, f32[64,128,64]{2,1,0:T(8,128)} %get-tuple-element.418, f32[64]{0:T(128)S(1)} %dynamic-slice_bitcast_fusion.2, pred[]{:T(512)S(6)} %compare.3, pred[]{:T(512)S(6)} %lt.51), kind=kLoop, calls=%fused_computation.4.clone.1 | loop fusion | flops 2097152 | bytes 6291714 | tf_op jit(solution)/shard_map/while/body/eval_jaxpr/jit(_where)/select_n | solution.py:28
  162.8 6.1 %fusion.43 = f32[64,128,64]{2,1,0:T(8,128)} fusion(f32[1,64,128,64]{3,2,1,0:T(8,128)} %copy.195, f32[64,128,64]{2,1,0:T(8,128)} %get-tuple-element.418, f32[64]{0:T(128)S(1)} %dynamic-slice_bitcast_fusion.2, pred[]{:T(512)S(6)} %compare.3, pred[]{:T(512)S(6)} %lt.51), kind=kLoop, calls=%fused_computation.4.clone.1 | loop fusion | flops 2097152 | bytes 6291714 | tf_op jit(solution)/shard_map/while/body/eval_jaxpr/jit(_where)/select_n | solution.py:28
  174.7 6.8 %fusion.43 = f32[64,128,64]{2,1,0:T(8,128)} fusion(f32[1,64,128,64]{3,2,1,0:T(8,128)} %copy.195, f32[64,128,64]{2,1,0:T(8,128)} %get-tuple-element.418, f32[64]{0:T(128)S(1)} %dynamic-slice_bitcast_fusion.2, pred[]{:T(512)S(6)} %compare.3, pred[]{:T(512)S(6)} %lt.51), kind=kLoop, calls=%fused_computation.4.clone.1 | loop fusion | flops 2097152 | bytes 6291714 | tf_op jit(solution)/shard_map/while/body/eval_jaxpr/jit(_where)/select_n | solution.py:28
  183.3 2.8 copy.195
  186.8 6.5 %fusion.43 = f32[64,128,64]{2,1,0:T(8,128)} fusion(f32[1,64,128,64]{3,2,1,0:T(8,128)} %copy.195, f32[64,128,64]{2,1,0:T(8,128)} %get-tuple-element.418, f32[64]{0:T(128)S(1)} %dynamic-slice_bitcast_fusion.2, pred[]{:T(512)S(6)} %compare.3, pred[]{:T(512)S(6)} %lt.51), kind=kLoop, calls=%fused_computation.4.clone.1 | loop fusion | flops 2097152 | bytes 6291714 | tf_op jit(solution)/shard_map/while/body/eval_jaxpr/jit(_where)/select_n | solution.py:28
  193.4 2.9 multiply_convert_fusion.2
  196.3 2.9 fusion.15
  199.2 8.2 %fusion.8 = f32[1,256,64,64]{1,3,2,0:T(8,128)} fusion(f32[4,16,64,256]{3,2,1,0:T(8,128)} %fusion.15, bf16[64,256,256]{2,1,0:T(8,128)(2,1)S(1)} %copy-done.1, f32[256,64]{0,1:T(8,128)S(1)} %copy.139, f32[256,64,64]{0,2,1:T(8,128)} %bitcast.133, f32[256,64]{0,1:T(8,128)S(1)} %get-tuple-element.338), kind=kOutput, calls=%fused_computation.22 | convolution fusion | flops 541065216 | bytes 21102592 | tf_op jit(solution)/shard_map/khij,kjhp->kihp/dot_general | solution.py:109
  207.3 5.8 %copy.145 = f32[256,4096]{1,0:T(8,128)} copy(f32[256,4096]{0,1:T(8,128)} %bitcast.141) | data formatting | bytes 8388608 | tf_op jit(solution)/shard_map/reshape | solution.py:133
  213.1 6.2 %add_multiply_fusion = f32[256,4096]{1,0:T(8,128)} fusion(f32[256,4096]{1,0:T(8,128)} %copy.145, f32[4096]{0:T(1024)S(1)} %mul.324, bf16[256,4096]{1,0:T(8,128)(2,1)} %param.18, bf16[256,4096]{1,0:T(8,128)(2,1)S(1)} %copy-done.8), kind=kLoop, calls=%fused_computation.29 | loop fusion | flops 9437184 | bytes 12599296 | tf_op jit(solution)/shard_map/mul | solution.py:138
  219.4 6.0 %reshape.335 = f32[256,4,1024]{2,1,0:T(4,128)} reshape(f32[256,4096]{1,0:T(8,128)} %add_multiply_fusion) | data formatting | bytes 8388608 | tf_op jit(solution)/shard_map/reshape | solution.py:138
  225.4 8.2 %fusion.19 = f32[256,4096]{1,0:T(8,128)S(1)} fusion(bf16[256,2048]{1,0:T(8,128)(2,1)S(1)} %copy-done, bf16[2048,4096]{1,0:T(8,128)(2,1)} %all-gather.8.cloned.1.call-done), kind=kOutput, calls=%fused_computation.71 | convolution fusion | flops 4294967296 | bytes 22020096 | tf_op jit(solution)/shard_map/dot_general | solution.py:161
  236.3 6.0 %reshape.336 = f32[256,4,1024]{2,1,0:T(4,128)} reshape(f32[256,4096]{1,0:T(8,128)} %fusion.4) | data formatting | bytes 8388608 | tf_op jit(solution)/shard_map/reshape | solution.py:164
  242.3 4.8 multiply_reduce_fusion.1
  247.7 5.8 %copy.175 = f32[32,8,4,1024]{3,1,2,0:T(8,128)} copy(f32[32,8,4,1024]{3,2,1,0:T(4,128)S(1)} %bitcast.142) | data formatting | bytes 8388608
  254.4 5.8 %copy.174 = f32[32,8,4,1024]{3,1,2,0:T(8,128)} copy(f32[32,8,4,1024]{3,2,1,0:T(4,128)S(1)} %bitcast.143) | data formatting | bytes 8388608
  261.0 4.2 copy.173
  265.2 6.4 %fusion.18 = (bf16[256,4096]{1,0:T(8,128)(2,1)}, f32[256,4096]{1,0:T(8,128)}, bf16[256,4096]{1,0:T(8,128)(2,1)S(1)}) fusion(bf16[256,4096]{1,0:T(8,128)(2,1)} %param.18, f32[256,4096]{1,0:T(8,128)S(1)} %bitcast.137, f32[256,4096]{1,0:T(8,128)S(1)} %copy-done.4, f32[256,4096]{1,0:T(8,128)} %bitcast.138, f32[256,4096]{1,0:T(8,128)S(1)} %bitcast.139, ...), kind=kLoop, calls=%fused_computation.70 | loop fusion | flops 15728640 | bytes 31473664 | tf_op jit(solution)/shard_map/convert_element_type | solution.py:169
  273.0 3.1 convolution_multiply_fusion.2
  276.3 3.8 fusion.2
  280.1 3.3 copy.151
  283.4 4.2 add_convert_fusion.1
  289.9 5.7 copy.156
  295.6 9.0 %all-gather.3 = bf16[8,1,64]{2,1,0:T(2,128)(2,1)S(1)} all-gather(bf16[1,1,64]{2,1,0:T(2,128)(2,1)S(1)} %copy-done.21), channel_id=5, replica_groups=mesh['dp'=16,'ctx'=8] {'ctx'}, dimensions={0}, use_global_device_ids=true | all-gather | bytes 1152 | tf_op jit(solution)/shard_map/all_gather | solution.py:38
  304.5 7.0 %fusion.20 = f32[64,64,256]{2,1,0:T(8,128)} fusion(bf16[256,64,64]{0,2,1:T(8,128)(2,1)S(1)} %bitcast.136, bf16[64,256,256]{2,1,0:T(8,128)(2,1)} %fusion.1), kind=kOutput, calls=%fused_computation.72 | convolution fusion | flops 536870912 | bytes 14680064 | tf_op jit(solution)/shard_map/khij,kihp->kjhp/dot_general | solution.py:170
  311.5 115.6 %all-reduce.3.cloned.1.call-done = (f32[64,4096]{1,0:T(8,128)}, f32[64,2048]{1,0:T(8,128)}) async-done(((f32[64,4096]{1,0:T(8,128)}, f32[64,2048]{1,0:T(8,128)}), (f32[64,4096]{1,0:T(8,128)}, f32[64,2048]{1,0:T(8,128)})) %all-reduce.3.cloned.1.call-update) | async-done | bytes 1572880 | tf_op jit(solution)/shard_map/psum | solution.py:195
  435.4 41.6 %all-gather.12.cloned.1.call-done = bf16[512,128,64]{1,2,0:T(8,128)(2,1)} async-done(((bf16[64,128,64]{1,2,0:T(8,128)(2,1)}), bf16[512,128,64]{1,2,0:T(8,128)(2,1)}) %all-gather.12.cloned.1.call-update) | async-done | bytes 8388624 | tf_op jit(solution)/shard_map/all_gather | solution.py:38
  479.5 62.9 %while.18 = (s32[]{:T(128)}, f32[64,128,64]{2,1,0:T(8,128)}, s32[]{:T(128)}, bf16[8,64]{1,0:T(8,128)(2,1)S(1)}, bf16[8,64,128,64]{2,3,1,0:T(8,128)(2,1)}, /*index=5*/s32[]{:T(128)}, s32[]{:T(128)}, s32[]{:T(128)}, s32[]{:T(128)}) while((s32[]{:T(128)}, f32[64,128,64]{2,1,0:T(8,128)}, s32[]{:T(128)}, bf16[8,64]{1,0:T(8,128)(2,1)S(1)}, ...), condition=%wide.region_7.8_spmd, body=%wide.region_6.7_spmd.sunk | while | flops 1572934 | bytes 9437979 | solution.py:53
  483.8 4.7 convert_add_fusion.2
  492.8 4.7 convert_add_fusion.2
  501.8 4.7 convert_add_fusion.2
  510.7 4.7 convert_add_fusion.2
  519.7 4.7 convert_add_fusion.2
  528.7 4.7 convert_add_fusion.2
  537.7 4.7 convert_add_fusion.2
  542.4 8.3 %convolution_add_fusion = f32[64,64,256]{2,1,0:T(8,128)} fusion(f32[64,64,256]{2,1,0:T(8,128)} %fusion.20, bf16[256,64,128]{2,0,1:T(8,128)(2,1)} %copy-done.2, f32[64,128,64]{2,1,0:T(8,128)} %get-tuple-element.212, f32[64]{0:T(128)S(1)} %copy-done.20), kind=kOutput, calls=%fused_computation.33 | convolution fusion | flops 270532608 | bytes 14680320 | tf_op jit(solution)/shard_map/kjhn,khnp->kjhp/dot_general | solution.py:188
  550.7 5.6 copy.157
  556.3 7.3 %add_convert_fusion = bf16[256,4096]{1,0:T(8,128)(2,1)} fusion(f32[256,4096]{1,0:T(8,128)} %get-tuple-element.334, f32[256,4096]{1,0:T(8,128)} %copy.156, f32[256,4096]{1,0:T(8,128)} %copy.157, f32[4096]{0:T(1024)S(1)} %mul.324), kind=kLoop, calls=%fused_computation.24 | loop fusion | flops 4194304 | bytes 14696448 | tf_op jit(solution)/shard_map/convert_element_type | solution.py:194
  (151 shorter events, 94.6 us)
Async XLA Ops:
  7.2 37.9 %copy-start = (bf16[256,2048]{1,0:T(8,128)(2,1)S(1)}, bf16[256,2048]{1,0:T(8,128)(2,1)}, u32[]{:S(2)}) copy-start(bf16[256,2048]{1,0:T(8,128)(2,1)} %param.29) | copy-start | bytes 3145732
  7.2 7.6 %copy-start.7 = (bf16[256,4096]{1,0:T(8,128)(2,1)S(1)}, bf16[256,4096]{1,0:T(8,128)(2,1)}, u32[]{:S(2)}) copy-start(bf16[256,4096]{1,0:T(8,128)(2,1)} %param.17) | copy-start | bytes 6291460
  7.2 106.1 %all-gather.10.cloned.1.call-start = ((), (), s32[]{:S(2)}) async-start(), calls=%async_computation.1 | async-start | bytes 18874368 | tf_op jit(solution)/shard_map/all_gather | solution.py:21
  10.7 0.6 copy-start.12
  11.9 9.7 %copy-start.23 = (f32[64]{0:T(128)}, f32[64]{0:T(128)S(1)}, u32[]{:S(2)}) copy-start(f32[64]{0:T(128)S(1)} %get-tuple-element.344) | copy-start | bytes 772
  17.7 5.8 %copy-start.3 = (f32[256,4096]{0,1:T(8,128)S(1)}, f32[256,4096]{0,1:T(8,128)}, u32[]{:S(2)}) copy-start(f32[256,4096]{0,1:T(8,128)} %copy.131) | copy-start | bytes 12582916
  21.6 1.9 copy-start.2
  23.5 3.2 copy-start.11
  23.5 3.3 copy-start.13
  23.5 3.4 copy-start.25
  23.5 3.6 copy-start.17
  23.5 4.2 copy-start.10
  25.8 199.6 %all-gather.8.cloned.1.call-start = ((), (), s32[]{:S(2)}) async-start(), calls=%async_computation | async-start | bytes 16908288 | tf_op jit(solution)/shard_map/all_gather | solution.py:160
  26.6 400.5 %all-reduce.3.cloned.1.call-start = ((), (), s32[]{:S(2)}) async-start(), calls=%async_computation.3 | async-start | bytes 3145728 | tf_op jit(solution)/shard_map/psum | solution.py:195
  28.1 5.7 copy-start.22
  28.1 16.9 %copy-start.16 = (bf16[64,2048]{1,0:T(8,128)(2,1)S(1)}, bf16[64,2048]{1,0:T(8,128)(2,1)}, u32[]{:S(2)}) copy-start(bf16[64,2048]{1,0:T(8,128)(2,1)} %param.27) | copy-start | bytes 786436
  193.4 5.8 %copy-start.1 = (bf16[64,256,256]{2,1,0:T(8,128)(2,1)S(1)}, bf16[64,256,256]{2,1,0:T(8,128)(2,1)}, u32[]{:S(2)}) copy-start(bf16[64,256,256]{2,1,0:T(8,128)(2,1)} %fusion.1) | copy-start | bytes 25165828
  207.3 5.8 %copy-start.8 = (bf16[256,4096]{1,0:T(8,128)(2,1)S(1)}, bf16[256,4096]{1,0:T(8,128)(2,1)}, u32[]{:S(2)}) copy-start(bf16[256,4096]{1,0:T(8,128)(2,1)} %param.17) | copy-start | bytes 6291460
  225.4 8.2 %copy-start.9 = (bf16[64,4096]{1,0:T(8,128)(2,1)S(1)}, bf16[64,4096]{1,0:T(8,128)(2,1)}, u32[]{:S(2)}) copy-start(bf16[64,4096]{1,0:T(8,128)(2,1)} %param.26) | copy-start | bytes 1572868
  225.4 8.2 %copy-start.14 = (bf16[256,64]{0,1:T(8,128)(2,1)S(1)}, bf16[256,64]{0,1:T(8,128)(2,1)}, u32[]{:S(2)}) copy-start(bf16[256,64]{0,1:T(8,128)(2,1)} %convolution_convert_fusion) | copy-start | bytes 98308
  236.3 6.0 %copy-start.19 = (f32[4,1024]{1,0:T(4,128)S(1)}, f32[4,1024]{1,0:T(4,128)}, u32[]{:S(2)}) copy-start(f32[4,1024]{1,0:T(4,128)} %mul.342) | copy-start | bytes 49156
  260.3 4.8 copy-start.6
  260.3 4.8 copy-start.18
  260.9 4.2 copy-start.4
  261.0 4.2 copy-start.5
  265.2 6.4 %copy-start.15 = (bf16[256,64]{0,1:T(8,128)(2,1)S(1)}, bf16[256,64]{0,1:T(8,128)(2,1)}, u32[]{:S(2)}) copy-start(bf16[256,64]{0,1:T(8,128)(2,1)} %convolution_convert_fusion) | copy-start | bytes 98308
  276.2 200.8 %all-gather.12.cloned.1.call-start = ((), (), s32[]{:S(2)}) async-start(), calls=%async_computation.2 | async-start | bytes 9437184 | tf_op jit(solution)/shard_map/all_gather | solution.py:38
  276.3 7.1 %copy-start.24 = (f32[64]{0:T(128)S(1)}, f32[64]{0:T(128)}, u32[]{:S(2)}) copy-start(f32[64]{0:T(128)} %copy-done.23) | copy-start | bytes 772
  289.9 5.7 copy-start.21
  479.5 62.9 %copy-start.20 = (f32[64]{0:T(128)S(1)}, f32[64]{0:T(128)}, u32[]{:S(2)}) copy-start(f32[64]{0:T(128)} %get-tuple-element.343) | copy-start | bytes 772
Sparse Core Ops, SparseCore 0:
  25.9 87.3 all-gather.9
  116.4 80.5 all-gather.7
  276.3 150.7 all-reduce.2
  429.2 47.7 all-gather.11
where the time goes:
time: 576 us; the launch traced here: 570 us
  waiting for transfers between devices  225 us (39%)
  local copies, waits for them, and re-layouts  132 us (23%)
  other arithmetic  127 us (22%)
  matrix products  49.5 us (9%)
  blocking collectives  20.2 us (4%)
  between operations  15.8 us (3%)
    psum x1, waiting for transfers between devices, on_device(): down_total, up_total = lax.psum((down_portion, up_portion), ('dp', 'ctx'))  116 us
    all_gather x1, waiting for transfers between devices, entering(): pieces = jax.tree.map(lambda part: lax.all_gather(part, axis), value)  67.2 us
    select_n x7, other arithmetic, lap(): jnp.where(position < mine, new, old)  43 us
    all_gather x1, waiting for transfers between devices, carried_in(): lax.all_gather(a.astype(kind), axis)  41.6 us
    add x7, other arithmetic, combine(): earlier[1] * later[0][:, None, None] + later[1]  32.7 us
    dynamic_slice x14, local copies, waits for them, and re-layouts, lap(): longer = join(running, jax.tree.map(lambda part: part[position], pieces))  32.2 us
    dynamic_slice x14, local copies, waits for them, and re-layouts, one(): lax.dynamic_index_in_dim(a, source, 0, False).astype(own.dtype)  30 us
    unnamed x58, local copies, waits for them, and re-layouts  19.1 us
  transfers between devices with their start and end apart: 4, of which 3 were waited for; matrix products, arithmetic and copies ran while one was open for 27% of the time, Pallas kernels for 0%

commit v1 on v0

v1 whole, which is shorter than its diff:
```python
import jax
import jax.numpy as jnp
from jax import lax
from jax.experimental import pallas as pl
from jax.experimental.pallas import tpu as pltpu
from jax.sharding import PartitionSpec as P

H = 64
P_SIZE = 64
N = 128
G = 4
Q = 256
INNER = 4096
OUTF = 2048
RANK = 64
GW = INNER // G
HG = H // G
PAIRS = HG // 2
EPS_NORM = 1e-05
CLIP_EPSILON = 1e-06
SCALE = 2.0
MESH = pl.DeviceIdType.MESH
F32 = jnp.float32
BF16 = jnp.bfloat16
VMEM_LIMIT = 62 * 1024 * 1024


def dot(a, b):
    return lax.dot_general(a, b, (((1,), (0,)), ((), ())), preferred_element_type=F32)


def dot_t(a, b):
    return lax.dot_general(a, b, (((1,), (1,)), ((), ())), preferred_element_type=F32)


def low_lanes(rows):
    return lax.broadcasted_iota(jnp.int32, (rows, 128), 1) < 64


def decay_tables(dtu_ref, bias_ref, alog_ref, cd_ref, cdt_ref):
    step = jax.nn.softplus(dtu_ref[...] + bias_ref[...])
    run = -jnp.exp(alog_ref[...]) * step
    rows = lax.broadcasted_iota(jnp.int32, (Q, H), 0)
    shift = 1
    while shift < Q:
        run = run + jnp.where(rows >= shift, pltpu.roll(run, shift, 0), 0.0)
        shift *= 2
    both = jnp.concatenate([run, step], axis=1)
    cd_ref[...] = both
    cdt_ref[...] = both.T


def group_tables(g, cd_ref, cdt_ref):
    cols = pltpu.roll(cd_ref[...], lax.rem(128 - HG * g, 128), 1)
    cum_rows = cdt_ref[pl.ds(pl.multiple_of(HG * g, 8), HG), :]
    return cols, cum_rows


def pair_lanes(cols, q, low):
    return jnp.where(low, cols[:, 2 * q : 2 * q + 1], cols[:, 2 * q + 1 : 2 * q + 2])


def forward_kernel(
    dtu_ref, bias_ref, alog_ref, skip_ref, x_ref, b_ref, c_ref, s_ref, tot_ref, y_ref, cd_ref, cdt_ref
):
    g = pl.program_id(0)

    @pl.when(g == 0)
    def _():
        decay_tables(dtu_ref, bias_ref, alog_ref, cd_ref, cdt_ref)

    cols, cum_rows = group_tables(g, cd_ref, cdt_ref)
    dts = cols[:, H : H + HG]
    low = low_lanes(Q)
    low_n = low_lanes(N)
    b_t = b_ref[...].astype(F32).T
    prod = dot_t(c_ref[...], b_ref[...])
    ri = lax.broadcasted_iota(jnp.int32, (128, 128), 0)
    ci = lax.broadcasted_iota(jnp.int32, (128, 128), 1)
    p00 = jnp.where(ri >= ci, prod[:128, :128], 0.0)
    p10 = prod[128:, :128]
    p11 = jnp.where(ri >= ci, prod[128:, 128:], 0.0)

    for q in range(PAIRS):
        xp = x_ref[:, q * 128 : (q + 1) * 128].astype(F32)
        xdt = (xp * pair_lanes(dts, q, low)).astype(BF16)
        tops, lows, states = [], [], []
        for h in (2 * q, 2 * q + 1):
            col = cols[:, h : h + 1]
            row = cum_rows[h : h + 1, :]
            s00 = (p00 * jnp.exp(jnp.minimum(col[:128] - row[:, :128], 0.0))).astype(BF16)
            s10 = (p10 * jnp.exp(jnp.minimum(col[128:] - row[:, :128], 0.0))).astype(BF16)
            s11 = (p11 * jnp.exp(jnp.minimum(col[128:] - row[:, 128:], 0.0))).astype(BF16)
            tops.append(dot(s00, xdt[:128]))
            lows.append(dot(jnp.concatenate([s10, s11], axis=1), xdt))
            bw = (b_t * jnp.exp(row[:, Q - 1 : Q] - row)).astype(BF16)
            states.append(dot(bw, xdt))
        skip = skip_ref[:, q * 128 : (q + 1) * 128]
        sl = slice(q * 128, (q + 1) * 128)
        y_ref[:128, sl] = jnp.where(low[:128], tops[0], tops[1]) + skip * xp[:128]
        y_ref[128:, sl] = jnp.where(low[:128], lows[0], lows[1]) + skip * xp[128:]
        s_ref[0, q] = jnp.where(low_n, states[0], states[1]).astype(BF16)
        tot_ref[0, q] = pair_lanes(cols[Q - 8 :, :HG], q, low_lanes(8))[7:8] + jnp.zeros((8, 128), F32)


def whole(shape):
    zeros = (0,) * len(shape)
    return pl.BlockSpec(shape, lambda g: zeros)


def local_forward(dtu, bias, alog, skip, x, b, c):
    col = lambda w: pl.BlockSpec((Q, w), lambda g: (0, g))
    return pl.pallas_call(
        forward_kernel,
        grid=(G,),
        in_specs=[
            whole((Q, H)),
            whole((1, H)),
            whole((1, H)),
            pl.BlockSpec((1, GW), lambda g: (0, g)),
            col(GW),
            col(N),
            col(N),
        ],
        out_specs=[
            pl.BlockSpec((1, PAIRS, N, 128), lambda g: (g, 0, 0, 0)),
            pl.BlockSpec((1, PAIRS, 8, 128), lambda g: (g, 0, 0, 0)),
            col(GW),
            whole((Q, 128)),
            whole((128, Q)),
        ],
        out_shape=[
            jax.ShapeDtypeStruct((G, PAIRS, N, 128), BF16),
            jax.ShapeDtypeStruct((G, PAIRS, 8, 128), F32),
            jax.ShapeDtypeStruct((Q, INNER), F32),
            jax.ShapeDtypeStruct((Q, 128), F32),
            jax.ShapeDtypeStruct((128, Q), F32),
        ],
        name="local_forward",
    )(dtu, bias, alog, skip, x, b, c)


class Place:
    def __init__(self):
        self.dp = lax.axis_index("dp")
        self.ctx = lax.axis_index("ctx")
        self.y = lax.div(self.dp, 4)
        self.z = lax.rem(self.dp, 4)
        self.x = lax.div(self.ctx, 2)
        self.c = lax.rem(self.ctx, 2)

    def coord(self, axis):
        return {"x": self.x, "y": self.y, "z": self.z}[axis]

    def along(self, axis, step):
        if axis == "x":
            return {"dp": self.dp, "ctx": lax.rem(self.x + step, 4) * 2 + self.c}
        if axis == "y":
            return {"dp": lax.rem(self.y + step, 4) * 4 + self.z, "ctx": self.ctx}
        return {"dp": self.y * 4 + lax.rem(self.z + step, 4), "ctx": self.ctx}

    def partner(self):
        return {"dp": self.dp, "ctx": self.x * 2 + 1 - self.c}

    def position(self, step):
        return lax.rem(self.ctx + step, 8)


def greet(devices):
    barrier = pltpu.get_barrier_semaphore()
    for device in devices:
        pl.semaphore_signal(barrier, inc=1, device_id=device, device_id_type=MESH)
    pl.semaphore_wait(barrier, len(devices))


def send(src, dst, sems, slot, device):
    copy = pltpu.make_async_remote_copy(
        src_ref=src,
        dst_ref=dst,
        send_sem=sems[0].at[slot],
        recv_sem=sems[1].at[slot],
        device_id=device,
        device_id_type=MESH,
    )
    copy.start()
    return copy


class Exchange:
    def __init__(self, place, s_ref, tot_ref, out_ref, got, got_tot, made, sems):
        self.place, self.s, self.tot, self.out = place, s_ref, tot_ref, out_ref
        self.got, self.got_tot, self.made, self.sems = got, got_tot, made, sems

    def scatter(self):
        me = self.place.ctx
        self.first = []
        for o in range(1, 8):
            k = self.place.position(o)
            device = {"dp": self.place.dp, "ctx": k}
            self.first.append(send(self.tot.at[:, k], self.got_tot.at[me], self.sems, 7 + o - 1, device))
            self.first.append(send(self.s.at[:, k], self.got.at[me], self.sems, o - 1, device))
        self.got[me] = self.s[:, me]
        self.got_tot[me] = self.tot[:, me]

    def combine(self, reverse):
        for copy in self.first:
            copy.wait()
        order = range(7, -1, -1) if reverse else range(8)
        for g in range(G):
            run = jnp.zeros((N, 128), F32)
            for j in order:
                self.made[j, g] = run.astype(BF16)
                run = jnp.exp(self.got_tot[j, g, 0:1]) * run + self.got[j, g].astype(F32)
        me = self.place.ctx
        self.second = []
        for o in range(1, 8):
            j = self.place.position(o)
            self.second.append(
                send(
                    self.made.at[j],
                    self.out.at[:, me],
                    self.sems,
                    14 + o - 1,
                    {"dp": self.place.dp, "ctx": j},
                )
            )
        self.out[:, me] = self.made[me]

    def finish(self):
        for copy in self.second:
            copy.wait()


EXCHANGE_SCRATCH = [
    pltpu.VMEM((8, G, N, 128), BF16),
    pltpu.VMEM((8, G, 8, 128), F32),
    pltpu.VMEM((8, G, N, 128), BF16),
    pltpu.SemaphoreType.DMA((21,)),
    pltpu.SemaphoreType.DMA((21,)),
]

PARTS = (
    (("x", "y", "z"), 0, 1664),
    (("y", "z", "x"), 1664, 768),
    (("x", "z", "y"), 2432, 1664),
)


class Part:
    def __init__(self, place, own_ref, out_ref, order, start, width, sems, base):
        self.place, self.own, self.out = place, own_ref, out_ref
        self.order, self.start, self.width = order, start, width
        self.first = (width // 128 + 1) // 2 * 128
        self.sems, self.slot = sems, base
        self.sent = []

    def view(self, stage, step, half=None):
        picks = {}
        for i, axis in enumerate(self.order):
            if i < stage:
                picks[axis] = slice(None)
            elif i == stage:
                picks[axis] = lax.rem(self.place.coord(axis) + step, 4)
            else:
                picks[axis] = self.place.coord(axis)
        c0, w = self.start, self.width
        if half == 0:
            w = self.first
        elif half == 1:
            c0, w = c0 + self.first, w - self.first
        return (picks["y"], picks["z"], picks["x"], self.place.c, slice(None), pl.ds(c0, w))

    def push(self, view, device, src=None):
        ref = self.out.at[view]
        copy = send(ref if src is None else src, ref, self.sems, self.slot, device)
        self.slot += 1
        self.sent.append(copy)
        return copy

    def hop_one(self, stage):
        axis = self.order[stage]
        view = self.view(stage, 0)
        src = None
        if stage == 0:
            src = self.own.at[:, pl.ds(self.start, self.width)]
        self.from_left = self.push(view, self.place.along(axis, 1), src)
        self.from_right = self.push(view, self.place.along(axis, 3), src)

    def hop_two(self, stage):
        axis = self.order[stage]
        self.from_left.wait_recv()
        far = [self.push(self.view(stage, 3, 0), self.place.along(axis, 1))]
        self.from_right.wait_recv()
        far.append(self.push(self.view(stage, 1, 1), self.place.along(axis, 3)))
        self.far = far

    def arrive(self):
        for copy in self.far:
            copy.wait_recv()

    def share(self, stage, step, half=None):
        return self.push(self.view(stage, step, half), self.place.partner())


SLOTS_PER_PART = 17


def gather_kernel(
    w_ref, s_ref, tot_ref, full_ref, inc_ref, got, got_tot, made, x_send, x_recv, send_sem, recv_sem, own_sem
):
    place = Place()
    near = [place.along(axis, step) for axis in "yz" for step in (1, 3)]
    greet(near + [{"dp": place.dp, "ctx": place.position(o)} for o in range(1, 8)])
    sems = (send_sem, recv_sem)
    parts = [
        Part(place, w_ref, full_ref, order, start, width, sems, i * SLOTS_PER_PART)
        for i, (order, start, width) in enumerate(PARTS)
    ]
    states = Exchange(place, s_ref, tot_ref, inc_ref, got, got_tot, made, (x_send, x_recv))
    own = pltpu.make_async_copy(w_ref, full_ref.at[place.y, place.z, place.x, place.c], own_sem)
    own.start()
    for part in parts:
        part.hop_one(0)
    states.scatter()
    for part in parts:
        part.hop_two(0)
    own.wait()
    for part in parts:
        part.arrive()
        part.hop_one(1)
    for part in parts:
        part.hop_two(1)
    for part in parts:
        part.arrive()
        part.hop_one(2)
    shared = [part.share(2, 0) for part in parts]
    states.combine(False)
    for part in parts:
        part.hop_two(2)
        shared.append(part.share(2, 3))
        shared.append(part.share(2, 1))
    for part in parts:
        part.arrive()
        shared.append(part.share(2, 2))
    for copy in shared:
        copy.wait_recv()
    for part in parts:
        for copy in part.sent:
            copy.wait_send()
    states.finish()


def gather_weight_and_states(w, s, tot):
    vmem = pl.BlockSpec(memory_space=pltpu.VMEM)
    return pl.pallas_call(
        gather_kernel,
        in_specs=[vmem, vmem, vmem],
        out_specs=[pl.BlockSpec(memory_space=pl.ANY), vmem],
        out_shape=[
            jax.ShapeDtypeStruct((4, 4, 4, 2, 16, INNER), BF16),
            jax.ShapeDtypeStruct((G, PAIRS, N, 128), BF16),
        ],
        scratch_shapes=EXCHANGE_SCRATCH
        + [
            pltpu.SemaphoreType.DMA((3 * SLOTS_PER_PART,)),
            pltpu.SemaphoreType.DMA((3 * SLOTS_PER_PART,)),
            pltpu.SemaphoreType.DMA,
        ],
        compiler_params=pltpu.CompilerParams(collective_id=1, has_side_effects=True),
        name="gather_weight_and_states",
    )(w, s, tot)


def reduce_kernel(
    g_ref,
    tot_ref,
    sa_ref,
    sb_ref,
    out_ref,
    da_ref,
    db_ref,
    got,
    got_tot,
    made,
    x_send,
    x_recv,
    a0,
    b0,
    a1,
    b1,
    ra1,
    rb1,
    a2,
    b2,
    ra2,
    rb2,
    ra3,
    rb3,
    sq,
    rsq,
    send_sem,
    recv_sem,
):
    place = Place()
    lines = [place.along(axis, step) for axis in "yz" for step in (1, 2, 3)]
    greet(lines + [{"dp": place.dp, "ctx": place.position(o)} for o in range(1, 8)])
    states = Exchange(place, g_ref, tot_ref, out_ref, got, got_tot, made, (x_send, x_recv))
    sems = (send_sem, recv_sem)
    slots = iter(range(64))
    push = lambda src, dst, device: send(src, dst, sems, next(slots), device)
    half = RANK // 2
    mine = pl.ds(pl.multiple_of(place.c * half, half), half)
    theirs = pl.ds(pl.multiple_of((1 - place.c) * half, half), half)
    partner = place.partner()

    first = [push(sa_ref.at[theirs], a0, partner), push(sb_ref.at[theirs], b0, partner)]
    states.scatter()
    for copy in first:
        copy.wait()
    a0[...] += sa_ref[mine]
    b0[...] += sb_ref[mine]

    def spread(axis, wide, narrow, a, b, ra, rb):
        copies = []
        for o in (1, 2, 3):
            to = lax.rem(place.coord(axis) + o, 4)
            device = place.along(axis, o)
            ca = pl.ds(pl.multiple_of(to * wide, 128), wide)
            cb = pl.ds(pl.multiple_of(to * narrow, 128), narrow)
            copies.append(push(a.at[:, ca], ra.at[o - 1], device))
            copies.append(push(b.at[:, cb], rb.at[o - 1], device))
        return copies

    def summed(axis, wide, narrow, a, b, ra, rb):
        own = place.coord(axis)
        ca = pl.ds(pl.multiple_of(own * wide, 128), wide)
        cb = pl.ds(pl.multiple_of(own * narrow, 128), narrow)
        return (
            a[:, ca] + (ra[0] + ra[1] + ra[2]),
            b[:, cb] + (rb[0] + rb[1] + rb[2]),
        )

    copies = spread("y", 1024, 512, a0, b0, ra1, rb1)
    states.combine(True)
    for copy in copies:
        copy.wait()
    a1[...], b1[...] = summed("y", 1024, 512, a0, b0, ra1, rb1)
    copies = spread("z", 256, 128, a1, b1, ra2, rb2)
    for copy in copies:
        copy.wait()
    a2[mine], b2[mine] = summed("z", 256, 128, a1, b1, ra2, rb2)
    copies = []
    for o in (1, 2, 3):
        device = place.along("x", o)
        copies.append(push(a2.at[mine], ra3.at[o - 1], device))
        copies.append(push(b2.at[mine], rb3.at[o - 1], device))
    for copy in copies:
        copy.wait()
    a2[mine] += ra3[0] + ra3[1] + ra3[2]
    b2[mine] += rb3[0] + rb3[1] + rb3[2]
    copies = [push(a2.at[mine], a2.at[mine], partner), push(b2.at[mine], b2.at[mine], partner)]
    for copy in copies:
        copy.wait()
    a = a2[...]
    b = b2[...]
    row = lax.broadcasted_iota(jnp.int32, (8, 128), 0)
    sq[0] = jnp.where(row == 0, jnp.sum(a * a), jnp.sum(b * b))
    for i, axis in enumerate("yz"):
        copies = [push(sq.at[i], rsq.at[i, o - 1], place.along(axis, o)) for o in (1, 2, 3)]
        for copy in copies:
            copy.wait()
        sq[i + 1] = sq[i] + (rsq[i, 0] + rsq[i, 1] + rsq[i, 2])
    total = sq[2]
    root_a = jnp.sqrt(total[0:1, 0:1] / (RANK * INNER) + CLIP_EPSILON)
    root_b = jnp.sqrt(total[1:2, 0:1] / (RANK * OUTF) + CLIP_EPSILON)
    da_ref[...] = a / jnp.maximum(1.0, root_a)
    db_ref[...] = b / jnp.maximum(1.0, root_b)
    states.finish()


def reduce_sums_and_states(grad, tot, sa, sb):
    vmem = pl.BlockSpec(memory_space=pltpu.VMEM)
    half = RANK // 2
    return pl.pallas_call(
        reduce_kernel,
        in_specs=[vmem] * 4,
        out_specs=[vmem] * 3,
        out_shape=[
            jax.ShapeDtypeStruct((G, PAIRS, N, 128), BF16),
            jax.ShapeDtypeStruct((RANK, 256), F32),
            jax.ShapeDtypeStruct((RANK, 128), F32),
        ],
        scratch_shapes=EXCHANGE_SCRATCH
        + [
            pltpu.VMEM((half, INNER), F32),
            pltpu.VMEM((half, OUTF), F32),
            pltpu.VMEM((half, 1024), F32),
            pltpu.VMEM((half, 512), F32),
            pltpu.VMEM((3, half, 1024), F32),
            pltpu.VMEM((3, half, 512), F32),
            pltpu.VMEM((RANK, 256), F32),
            pltpu.VMEM((RANK, 128), F32),
            pltpu.VMEM((3, half, 256), F32),
            pltpu.VMEM((3, half, 128), F32),
            pltpu.VMEM((3, half, 256), F32),
            pltpu.VMEM((3, half, 128), F32),
            pltpu.VMEM((3, 8, 128), F32),
            pltpu.VMEM((2, 3, 8, 128), F32),
            pltpu.SemaphoreType.DMA((32,)),
            pltpu.SemaphoreType.DMA((32,)),
        ],
        compiler_params=pltpu.CompilerParams(collective_id=2, has_side_effects=True),
        name="reduce_sums_and_states",
    )(grad, tot, sa, sb)


def middle_kernel(
    y_ref,
    z_ref,
    c_ref,
    inc_ref,
    cd_ref,
    cdt_ref,
    gain_ref,
    w_ref,
    cot_ref,
    down_ref,
    up_ref,
    d_ref,
    grad_ref,
    sa_ref,
    sb_ref,
    ssd,
    dn,
    normed,
    up_t,
    up_row,
    down_t,
):
    g = pl.program_id(0)

    @pl.when(g == 0)
    def _():
        up_t[...] = dot_t(up_ref[...], cot_ref[...]).astype(BF16)
        up_row[...] = dot_t(cot_ref[...], up_ref[...]).astype(BF16)
        down_t[...] = jnp.zeros_like(down_t)

    cols, cum_rows = group_tables(g, cd_ref, cdt_ref)
    grow = jnp.exp(cols[:, :HG])
    low = low_lanes(Q)
    low_n = low_lanes(N)
    cg = c_ref[...]
    for q in range(PAIRS):
        sl = slice(q * 128, (q + 1) * 128)
        ssd[:, sl] = y_ref[:, sl] + pair_lanes(grow, q, low) * dot(cg, inc_ref[0, q])
    for i in range(GW // 256):
        sl = slice(i * 256, (i + 1) * 256)
        dn[:, sl] = dot(cot_ref[...], w_ref[:, sl]) + SCALE * dot(up_row[...], down_ref[:, sl])

    gain = gain_ref[...]
    rows = 16

    def chunk(i, carry):
        at = pl.ds(pl.multiple_of(i * rows, rows), rows)
        zf = z_ref[at, :].astype(F32)
        silu = zf / (1.0 + jnp.exp(-zf))
        gated = ssd[at, :] * silu
        rstd = lax.rsqrt(jnp.mean(gated * gated, axis=-1, keepdims=True) + EPS_NORM)
        hat = gated * rstd
        normed[at, :] = (hat * gain).astype(BF16)
        wg = dn[at, :] * gain
        slope = jnp.mean(hat * wg, axis=-1, keepdims=True)
        d_ref[at, :] = (rstd * (wg - hat * slope) * silu).astype(BF16)
        return carry

    lax.fori_loop(0, Q // rows, chunk, 0)

    c_t = cg.astype(F32).T
    for q in range(PAIRS):
        dp = d_ref[:, q * 128 : (q + 1) * 128]
        halves = []
        for h in (2 * q, 2 * q + 1):
            cw = (c_t * jnp.exp(cum_rows[h : h + 1, :])).astype(BF16)
            halves.append(dot(cw, dp))
        grad_ref[0, q] = jnp.where(low_n, halves[0], halves[1]).astype(BF16)
    sa_ref[...] = SCALE * dot(up_t[...], normed[...])
    down_t[...] += dot_t(down_ref[...], normed[...])

    @pl.when(g == G - 1)
    def _():
        sb_ref[...] = SCALE * dot(down_t[...].astype(BF16), cot_ref[...])


def middle(y, z, c, inc, cd, cdt, gain, w, cot, down, up):
    col = lambda w_: pl.BlockSpec((Q, w_), lambda g: (0, g))
    return pl.pallas_call(
        middle_kernel,
        grid=(G,),
        in_specs=[
            col(GW),
            col(GW),
            col(N),
            pl.BlockSpec((1, PAIRS, N, 128), lambda g: (g, 0, 0, 0)),
            whole((Q, 128)),
            whole((128, Q)),
            pl.BlockSpec((1, GW), lambda g: (0, g)),
            pl.BlockSpec((OUTF, GW), lambda g: (0, g)),
            whole((Q, OUTF)),
            pl.BlockSpec((RANK, GW), lambda g: (0, g)),
            whole((RANK, OUTF)),
        ],
        out_specs=[
            col(GW),
            pl.BlockSpec((1, PAIRS, N, 128), lambda g: (g, 0, 0, 0)),
            pl.BlockSpec((RANK, GW), lambda g: (0, g)),
            whole((RANK, OUTF)),
        ],
        out_shape=[
            jax.ShapeDtypeStruct((Q, INNER), BF16),
            jax.ShapeDtypeStruct((G, PAIRS, N, 128), BF16),
            jax.ShapeDtypeStruct((RANK, INNER), F32),
            jax.ShapeDtypeStruct((RANK, OUTF), F32),
        ],
        scratch_shapes=[
            pltpu.VMEM((Q, GW), F32),
            pltpu.VMEM((Q, GW), F32),
            pltpu.VMEM((Q, GW), BF16),
            pltpu.VMEM((RANK, Q), BF16),
            pltpu.VMEM((Q, RANK), BF16),
            pltpu.VMEM((RANK, Q), F32),
        ],
        compiler_params=pltpu.CompilerParams(vmem_limit_bytes=48 * 1024 * 1024),
        name="middle",
    )(y, z, c, inc, cd, cdt, gain, w, cot, down, up)


def backward_kernel(d_ref, b_ref, c_ref, outg_ref, cd_ref, cdt_ref, skip_ref, o_ref):
    g = pl.program_id(0)
    cols, cum_rows = group_tables(g, cd_ref, cdt_ref)
    dts = cols[:, H : H + HG]
    fade = jnp.exp(cols[Q - 1 : Q, :HG] - cols[:, :HG])
    low = low_lanes(Q)
    bg = b_ref[...]
    prod = dot_t(bg, c_ref[...])
    ri = lax.broadcasted_iota(jnp.int32, (128, 128), 0)
    ci = lax.broadcasted_iota(jnp.int32, (128, 128), 1)
    p00 = jnp.where(ci >= ri, prod[:128, :128], 0.0)
    p01 = prod[:128, 128:]
    p11 = jnp.where(ci >= ri, prod[128:, 128:], 0.0)
    for q in range(PAIRS):
        sl = slice(q * 128, (q + 1) * 128)
        dp = d_ref[:, sl]
        tops, lows = [], []
        for h in (2 * q, 2 * q + 1):
            col = cols[:, h : h + 1]
            row = cum_rows[h : h + 1, :]
            s00 = (p00 * jnp.exp(jnp.minimum(row[:, :128] - col[:128], 0.0))).astype(BF16)
            s01 = (p01 * jnp.exp(jnp.minimum(row[:, 128:] - col[:128], 0.0))).astype(BF16)
            s11 = (p11 * jnp.exp(jnp.minimum(row[:, 128:] - col[128:], 0.0))).astype(BF16)
            tops.append(dot(jnp.concatenate([s00, s01], axis=1), dp))
            lows.append(dot(s11, dp[128:]))
        cross = pair_lanes(fade, q, low) * dot(bg, outg_ref[0, q])
        dt = pair_lanes(dts, q, low)
        skip = skip_ref[:, sl]
        top = jnp.where(low[:128], tops[0], tops[1]) + cross[:128]
        bottom = jnp.where(low[:128], lows[0], lows[1]) + cross[128:]
        o_ref[:128, sl] = (dt[:128] * top + skip * dp[:128].astype(F32)).astype(BF16)
        o_ref[128:, sl] = (dt[128:] * bottom + skip * dp[128:].astype(F32)).astype(BF16)


def local_backward(d, b, c, outg, cd, cdt, skip):
    col = lambda w: pl.BlockSpec((Q, w), lambda g: (0, g))
    return pl.pallas_call(
        backward_kernel,
        grid=(G,),
        in_specs=[
            col(GW),
            col(N),
            col(N),
            pl.BlockSpec((1, PAIRS, N, 128), lambda g: (g, 0, 0, 0)),
            whole((Q, 128)),
            whole((128, Q)),
            pl.BlockSpec((1, GW), lambda g: (0, g)),
        ],
        out_specs=col(GW),
        out_shape=jax.ShapeDtypeStruct((Q, INNER), BF16),
        name="local_backward",
    )(d, b, c, outg, cd, cdt, skip)


def on_device(x, z, b, c, dtu, bias, alog, skip, gain, down, up, w, cot):
    skip_cols = jnp.broadcast_to(skip[:, None], (H, P_SIZE)).reshape(1, INNER)
    s, tot, y, cd, cdt = local_forward(
        dtu, bias.reshape(1, H), alog.reshape(1, H), skip_cols, x, b, c
    )
    full, inc = gather_weight_and_states(w, s, tot)
    d, grad, sa, sb = middle(
        y, z, c, inc, cd, cdt, gain.reshape(1, INNER), full.reshape(OUTF, INNER), cot, down, up
    )
    outg, da, db = reduce_sums_and_states(grad, tot, sa, sb)
    dx = local_backward(d, b, c, outg, cd, cdt, skip_cols)
    place = lax.axis_index("ctx")
    da = lax.dynamic_slice_in_dim(da, place * 32, 32, 1)
    db = lax.dynamic_slice_in_dim(db, place * 16, 16, 1)
    return dx, da, db


def solution(mesh):
    rows = P(("dp", "ctx"), None)
    placed = (rows,) * 5 + (P(),) * 6 + (rows, rows)
    return jax.shard_map(
        on_device,
        mesh=mesh,
        in_specs=placed,
        out_specs=(rows, P(None, ("dp", "ctx")), P(None, ("dp", "ctx"))),
        check_vma=False,
    )
```

time: 576 us -> 177 us (0.31)
  waiting for transfers between devices: 225 us -> 0 us
  Pallas kernels: 0 us -> 166 us
  other arithmetic: 127 us -> 0 us
  local copies, waits for them, and re-layouts: 132 us -> 10.3 us
  matrix products: 49.5 us -> 0 us
  blocking collectives: 20.2 us -> 0 us
  between operations: 15.8 us -> 0.74 us
    pallas_call x0 -> x5, Pallas kernels: none -> 166 us  [the longest x1 72.2 us: gather_weight_and_states(): pl.pallas_call(gather_kernel, in_specs=[vmem, vmem, vmem], out_specs=[pl....]
    psum x1 -> x0, waiting for transfers between devices: 116 us -> none  [on_device(): down_total, up_total = lax.psum((down_portion, up_portion), ('dp', 'ctx'))]
    all_gather x3 -> x0, waiting for transfers between devices: 109 us -> none  [the longest x1 67.2 us: entering(): pieces = jax.tree.map(lambda part: lax.all_gather(part, axis), value)]
    dynamic_slice x28 -> x2, local copies, waits for them, and re-layouts: 62.2 us -> 0.15 us  [the longest x1 0.08 us: on_device(): da = lax.dynamic_slice_in_dim(da, place * 32, 32, 1)]
    dot_general x12 -> x0, matrix products: 49.5 us -> none  [the longest x1 8.33 us: on_device(): jnp.einsum('kjhn,khnp->kjhp', b_weighted, outgoing_bf, preferred_element_...]
    select_n x7 -> x0, other arithmetic: 43 us -> none  [lap(): jnp.where(position < mine, new, old)]
    add x7 -> x0, other arithmetic: 32.7 us -> none  [combine(): earlier[1] * later[0][:, None, None] + later[1]]
    convert_element_type x14 -> x0, other arithmetic: 30.6 us -> none  [the longest x1 7.27 us: on_device(): grad_heads.reshape(row_count, INNER_CHANNELS).astype(jnp.bfloat16)]
  transfers between devices with their start and end apart: 4 -> 0, of which waited for: 3 -> 0; matrix products, arithmetic and copies ran while one was open for 27% -> 0% of each run, Pallas kernels for 0% -> 0%
where the time goes in v1:
time: 177 us
  Pallas kernels  166 us (94%)
  local copies, waits for them, and re-layouts  10.3 us (6%)
    pallas_call x1, Pallas kernels, gather_weight_and_states(): pl.pallas_call(gather_kernel, in_specs=[vmem, vmem, vmem], out_specs=[pl....  72.2 us
    pallas_call x1, Pallas kernels, reduce_sums_and_states(): pl.pallas_call(reduce_kernel, in_specs=[vmem] * 4, out_specs=[vmem] * 3,...  45.4 us
    pallas_call x1, Pallas kernels, middle(): pl.pallas_call(middle_kernel, grid=(G,), in_specs=[col(GW), col(GW), col(...  27.6 us
    pallas_call x1, Pallas kernels, local_backward(): pl.pallas_call(backward_kernel, grid=(G,), in_specs=[col(GW), col(N), col...  10.5 us
    pallas_call x1, Pallas kernels, local_forward(): pl.pallas_call(forward_kernel, grid=(G,), in_specs=[whole((Q, H)), whole(...  9.93 us
    unnamed x29, local copies, waits for them, and re-layouts  8.78 us

profile of v1, /device:TPU:0, one launch (start us, length us, event | category | flops | bytes accessed | tf_op | source)
XLA Modules:
  0.0 176.7 jit_solution(16839294922329968261)
XLA Ops:
  0.6 0.7 broadcast_in_dim.2
  1.4 0.7 reshape.24.skip_ref
  2.1 1.6 copy.16.dtu_ref
  3.6 0.0 copy-start
  3.6 0.0 copy-start.1
  3.6 0.0 copy-start.7
  3.7 0.0 copy-start.9
  3.7 0.0 copy-start.10
  3.7 9.9 %local_forward.1 = (bf16[4,8,128,128]{3,2,1,0:T(8,128)(2,1)}, f32[4,8,8,128]{3,2,1,0:T(8,128)}, f32[256,4096]{1,0:T(8,128)}, f32[256,128]{1,0:T(8,128)}, f32[128,256]{1,0:T(8,128)}) custom-call(f32[256,64]{1,0:T(8,128)} %copy.16.dtu_ref, f32[1,64]{1,0:T(1,128)} %bitcast.6, f32[1,64]{1,0:T(1,128)} %bitcast.7, f32[1,4096]{1,0:T(1,128)} %reshape.24.skip_ref, ...), custom_call_target="tpu_custom_call" | custom-call | tf_op jit(solution)/shard_map/local_forward/pallas_call | solution.py:113
  13.6 72.2 %gather_weight_and_states.1 = (bf16[4,4,4,2,16,4096]{5,4,3,2,1,0:T(8,128)(2,1)}, bf16[4,8,128,128]{3,2,1,0:T(8,128)(2,1)}) custom-call(bf16[16,4096]{1,0:T(8,128)(2,1)} %w_ref.1, bf16[4,8,128,128]{3,2,1,0:T(8,128)(2,1)} %get-tuple-element.18.s_ref, f32[4,8,8,128]{3,2,1,0:T(8,128)} %get-tuple-element.19.tot_ref), custom_call_target="tpu_custom_call" | custom-call | tf_op jit(solution)/shard_map/gather_weight_and_states/pallas_call | solution.py:355
  85.8 0.0 copy-done
  85.8 0.0 copy-done.1
  85.8 0.0 copy-done.7
  85.8 0.0 copy-done.9
  85.8 0.0 copy-done.10
  85.8 0.0 copy-start.2
  85.8 1.2 copy-done.2
  87.0 0.0 copy-start.5
  87.0 0.9 copy-done.5
  87.9 0.0 copy-start.6
  87.9 0.9 copy-done.6
  88.8 27.6 %middle.1 = (bf16[256,4096]{1,0:T(8,128)(2,1)}, bf16[4,8,128,128]{3,2,1,0:T(8,128)(2,1)S(1)}, f32[64,4096]{1,0:T(8,128)S(1)}, f32[64,2048]{1,0:T(8,128)S(1)}) custom-call(f32[256,4096]{1,0:T(8,128)} %get-tuple-element.17.y_ref, bf16[256,4096]{1,0:T(8,128)(2,1)} %z_ref.1, bf16[256,512]{1,0:T(8,128)(2,1)S(1)} %copy-done, ...), custom_call_target="tpu_custom_call" | custom-call | tf_op jit(solution)/shard_map/middle/pallas_call | solution.py:596
  116.4 0.0 copy-start.3
  116.4 1.0 copy-done.3
  117.4 0.0 copy-start.4
  117.4 1.0 copy-done.4
  118.4 0.0 copy-start.8
  118.4 0.8 copy-done.8
  119.2 45.4 %reduce_sums_and_states.1 = (bf16[4,8,128,128]{3,2,1,0:T(8,128)(2,1)}, f32[64,256]{1,0:T(8,128)}, f32[64,128]{1,0:T(8,128)}) custom-call(bf16[4,8,128,128]{3,2,1,0:T(8,128)(2,1)} %copy-done.3, f32[4,8,8,128]{3,2,1,0:T(8,128)} %get-tuple-element.19.tot_ref, f32[64,4096]{1,0:T(8,128)} %copy-done.4, f32[64,2048]{1,0:T(8,128)} %copy-done.8), custom_call_target="tpu_custom_call" | custom-call | tf_op jit(solution)/shard_map/reduce_sums_and_states/pallas_call | solution.py:484
  164.6 0.0 copy-start.12
  164.6 0.0 copy-start.11
  164.6 10.5 %local_backward.1 = bf16[256,4096]{1,0:T(8,128)(2,1)} custom-call(bf16[256,4096]{1,0:T(8,128)(2,1)} %get-tuple-element.24.d_ref, bf16[256,512]{1,0:T(8,128)(2,1)} %b_ref.3, bf16[256,512]{1,0:T(8,128)(2,1)} %c_ref.5, bf16[4,8,128,128]{3,2,1,0:T(8,128)(2,1)} %get-tuple-element.28.outg_ref, f32[256,128]{1,0:T(8,128)} %get-tuple-element.21.cd_ref, ...), custom_call_target="tpu_custom_call" | custom-call | tf_op jit(solution)/shard_map/local_backward/pallas_call | solution.py:673
  175.2 0.0 copy-done.12
  175.2 0.1 constant_dynamic-slice_fusion.1
  175.2 0.7 copy.17
  175.9 0.0 copy-done.11
  175.9 0.1 constant_dynamic-slice_fusion
  176.0 0.7 copy.18
Async XLA Ops:
  3.6 82.1 %copy-start = (bf16[256,512]{1,0:T(8,128)(2,1)S(1)}, bf16[256,512]{1,0:T(8,128)(2,1)}, u32[]{:S(2)}) copy-start(bf16[256,512]{1,0:T(8,128)(2,1)} %c_ref.5) | copy-start | bytes 786436
  3.6 82.1 %copy-start.1 = (bf16[256,2048]{1,0:T(8,128)(2,1)S(1)}, bf16[256,2048]{1,0:T(8,128)(2,1)}, u32[]{:S(2)}) copy-start(bf16[256,2048]{1,0:T(8,128)(2,1)} %cot_ref.1) | copy-start | bytes 3145732
  3.6 82.1 %copy-start.7 = (bf16[64,4096]{1,0:T(8,128)(2,1)S(1)}, bf16[64,4096]{1,0:T(8,128)(2,1)}, u32[]{:S(2)}) copy-start(bf16[64,4096]{1,0:T(8,128)(2,1)} %down_ref.1) | copy-start | bytes 1572868
  3.7 82.1 %copy-start.9 = (bf16[64,2048]{1,0:T(8,128)(2,1)S(1)}, bf16[64,2048]{1,0:T(8,128)(2,1)}, u32[]{:S(2)}) copy-start(bf16[64,2048]{1,0:T(8,128)(2,1)} %up_ref.1) | copy-start | bytes 786436
  3.7 82.2 %copy-start.10 = (f32[4096]{0:T(1024)S(1)}, f32[4096]{0:T(1024)}, u32[]{:S(2)}) copy-start(f32[4096]{0:T(1024)} %param.21) | copy-start | bytes 49156
  85.8 1.2 copy-start.2
  87.0 0.9 copy-start.5
  87.9 0.9 copy-start.6
  116.4 1.0 copy-start.3
  117.4 1.0 copy-start.4
  118.4 0.8 copy-start.8
  164.6 10.5 %copy-start.12 = (f32[64,256]{1,0:T(8,128)S(1)}, f32[64,256]{1,0:T(8,128)}, u32[]{:S(2)}) copy-start(f32[64,256]{1,0:T(8,128)} %get-tuple-element.29) | copy-start | bytes 196612
  164.6 11.3 %copy-start.11 = (f32[64,128]{1,0:T(8,128)S(1)}, f32[64,128]{1,0:T(8,128)}, u32[]{:S(2)}) copy-start(f32[64,128]{1,0:T(8,128)} %get-tuple-element.30) | copy-start | bytes 98308

commit v2 on v0

v2 whole, which is shorter than its diff:
```python
import jax
import jax.numpy as jnp
from jax import lax
from jax.experimental import pallas as pl
from jax.experimental.pallas import tpu as pltpu
from jax.sharding import PartitionSpec as P

H = 64
P_SIZE = 64
N = 128
G = 4
Q = 256
INNER = 4096
OUTF = 2048
RANK = 64
GW = INNER // G
HG = H // G
PAIRS = HG // 2
EPS_NORM = 1e-05
CLIP_EPSILON = 1e-06
SCALE = 2.0
MESH = pl.DeviceIdType.MESH
F32 = jnp.float32
BF16 = jnp.bfloat16
VMEM_LIMIT = 62 * 1024 * 1024


def dot(a, b):
    return lax.dot_general(a, b, (((1,), (0,)), ((), ())), preferred_element_type=F32)


def dot_t(a, b):
    return lax.dot_general(a, b, (((1,), (1,)), ((), ())), preferred_element_type=F32)


def low_lanes(rows):
    return lax.broadcasted_iota(jnp.int32, (rows, 128), 1) < 64


def pair_cols(cd_ref, p):
    return pltpu.roll(cd_ref[...], lax.rem(128 - 2 * p, 128), 1)


def pair_lanes(cols, at, low):
    return jnp.where(low, cols[:, at : at + 1], cols[:, at + 1 : at + 2])


def lanes_at(p):
    return pl.ds(pl.multiple_of(p * 128, 128), 128)


class Place:
    def __init__(self):
        self.dp = lax.axis_index("dp")
        self.ctx = lax.axis_index("ctx")
        self.y = lax.div(self.dp, 4)
        self.z = lax.rem(self.dp, 4)
        self.x = lax.div(self.ctx, 2)
        self.c = lax.rem(self.ctx, 2)

    def coord(self, axis):
        return {"x": self.x, "y": self.y, "z": self.z}[axis]

    def along(self, axis, step):
        if axis == "x":
            return {"dp": self.dp, "ctx": lax.rem(self.x + step, 4) * 2 + self.c}
        if axis == "y":
            return {"dp": lax.rem(self.y + step, 4) * 4 + self.z, "ctx": self.ctx}
        return {"dp": self.y * 4 + lax.rem(self.z + step, 4), "ctx": self.ctx}

    def partner(self):
        return {"dp": self.dp, "ctx": self.x * 2 + 1 - self.c}

    def position(self, step):
        return lax.rem(self.ctx + step, 8)


def greet(devices):
    barrier = pltpu.get_barrier_semaphore()
    for device in devices:
        pl.semaphore_signal(barrier, inc=1, device_id=device, device_id_type=MESH)
    return lambda: pl.semaphore_wait(barrier, len(devices))


class Link:
    def __init__(self, send_sem, recv_sem):
        self.send_sem, self.recv_sem, self.used, self.sent = send_sem, recv_sem, 0, []

    def push(self, src, dst, device):
        copy = pltpu.make_async_remote_copy(
            src_ref=src,
            dst_ref=dst,
            send_sem=self.send_sem.at[self.used],
            recv_sem=self.recv_sem.at[self.used],
            device_id=device,
            device_id_type=MESH,
        )
        self.used += 1
        copy.start()
        self.sent.append(copy)
        return copy

    def settle(self, copies):
        for copy in copies:
            copy.wait_send()
        self.sent = [old for old in self.sent if all(old is not copy for copy in copies)]

    def drain(self):
        for copy in self.sent:
            copy.wait_send()


class Exchange:
    def __init__(self, place, link, own, tots, got, made, out, reverse):
        self.place, self.link, self.own, self.tots = place, link, own, tots
        self.got, self.made, self.out, self.reverse = got, made, out, reverse
        self.first, self.second = {}, {}

    def peer(self, k):
        return {"dp": self.place.dp, "ctx": k}

    def scatter(self, g):
        me = self.place.ctx
        self.first[g] = []
        for o in range(1, 8):
            k = self.place.position(o)
            self.first[g].append(self.link.push(self.own.at[g, k], self.got.at[me, g], self.peer(k)))
        self.got[me, g] = self.own[g, me]

    def combine(self, g):
        for copy in self.first[g]:
            copy.wait_recv()
        run = jnp.zeros((N, 128), F32)
        for j in range(7, -1, -1) if self.reverse else range(8):
            self.made[j, g] = run.astype(BF16)
            run = jnp.exp(self.tots[j, g, 0:1]) * run + self.got[j, g].astype(F32)
        me = self.place.ctx
        self.second[g] = []
        for o in range(1, 8):
            j = self.place.position(o)
            self.second[g].append(self.link.push(self.made.at[j, g], self.out.at[g, me], self.peer(j)))
        self.out[g, me] = self.made[me, g]

    def finish(self, g):
        for copy in self.second[g]:
            copy.wait_recv()


PARTS = (
    (("x", "y", "z"), 0, 3),
    (("y", "z", "x"), 3, 2),
    (("x", "z", "y"), 5, 3),
)


class Part:
    def __init__(self, place, link, buf, order, start, tiles):
        self.place, self.link, self.buf = place, link, buf
        self.order, self.start, self.tiles = order, start, tiles
        self.near, self.far = {}, {}

    def view(self, stage, step, group=None, groups=None, tiles=None):
        picks = {}
        for i, axis in enumerate(self.order):
            if i < stage:
                picks[axis] = slice(None)
            elif i == stage:
                picks[axis] = lax.rem(self.place.coord(axis) + step, 4)
            else:
                picks[axis] = self.place.coord(axis)
        lo, count = (0, self.tiles) if tiles is None else tiles
        where = groups if group is None else group
        if where is None:
            where = slice(None)
        return self.buf.at[
            picks["y"],
            picks["z"],
            picks["x"],
            self.place.c,
            where,
            slice(None),
            pl.ds((self.start + lo) * 128, count * 128),
        ]

    def push(self, view, device):
        return self.link.push(view, view, device)

    def hop_one(self, stage, g=None):
        axis = self.order[stage]
        view = self.view(stage, 0, g)
        self.near[stage, g] = (
            self.push(view, self.place.along(axis, 1)),
            self.push(view, self.place.along(axis, 3)),
        )

    def cut(self, g):
        if g is None:
            return {"groups": slice(0, 2)}, {"groups": slice(2, 4)}
        lo = (self.tiles + 1 - g % 2) // 2
        low = {"group": g, "tiles": (0, lo)} if lo else None
        high = {"group": g, "tiles": (lo, self.tiles - lo)} if lo < self.tiles else None
        return low, high

    def hop_two(self, stage, g=None):
        axis = self.order[stage]
        low, high = self.cut(g)
        left, right = self.near[stage, g]
        self.far[stage, g] = []
        left.wait_recv()
        if low is not None:
            self.far[stage, g].append(self.push(self.view(stage, 3, **low), self.place.along(axis, 1)))
        right.wait_recv()
        if high is not None:
            self.far[stage, g].append(self.push(self.view(stage, 1, **high), self.place.along(axis, 3)))

    def arrive(self, stage, g=None):
        for copy in self.far[stage, g]:
            copy.wait_recv()

    def share(self, step, g):
        return self.push(self.view(2, step, g), self.place.partner())


class Weight:
    def __init__(self, place, link, buf):
        self.parts = [Part(place, link, buf, *part) for part in PARTS]
        self.shared = {g: [] for g in range(G)}
        self.plan = (
            (lambda: self.one(0, None),),
            (lambda: self.two(0, None),),
            (lambda: self.one(1, 0, (0, None)), lambda: self.one(1, 1)),
            (lambda: self.two(1, 0), lambda: self.one(1, 2)),
            (lambda: self.last(0), lambda: self.two(1, 1), lambda: self.one(1, 3)),
            (lambda: self.last(1), lambda: self.two(1, 2)),
            (lambda: self.relay(0), lambda: self.last(2), lambda: self.two(1, 3)),
            (lambda: self.relay(1), lambda: self.last(3)),
            (lambda: self.land(0), lambda: self.relay(2)),
            (lambda: self.land(1), lambda: self.relay(3)),
            (lambda: self.land(2),),
            (lambda: self.land(3),),
        )
        self.at = 0

    def step(self):
        for act in self.plan[self.at]:
            act()
        self.at += 1

    def one(self, stage, g, after=None):
        for part in self.parts:
            if after is not None:
                part.arrive(*after)
            part.hop_one(stage, g)

    def two(self, stage, g):
        for part in self.parts:
            part.hop_two(stage, g)

    def last(self, g):
        self.one(2, g, (1, g))
        for part in self.parts:
            self.shared[g].append(part.share(0, g))

    def relay(self, g):
        for part in self.parts:
            part.hop_two(2, g)
        for part in self.parts:
            self.shared[g].append(part.share(3, g))
            self.shared[g].append(part.share(1, g))

    def land(self, g):
        for part in self.parts:
            part.arrive(2, g)
            self.shared[g].append(part.share(2, g))

    def ready(self, g):
        for copy in self.shared[g]:
            copy.wait_recv()


class Sums:
    def __init__(self, place, link, sa, sb, da, db, bufs):
        self.place, self.link, self.sa, self.sb, self.da, self.db = place, link, sa, sb, da, db
        self.bufs = bufs

    def spread(self, axis, wide, narrow, a, b, ra, rb):
        copies = []
        for o in (1, 2, 3):
            to = lax.rem(self.place.coord(axis) + o, 4)
            device = self.place.along(axis, o)
            ca = pl.ds(pl.multiple_of(to * wide, 128), wide)
            cb = pl.ds(pl.multiple_of(to * narrow, 128), narrow)
            copies.append(self.link.push(a.at[:, ca], ra.at[o - 1], device))
            copies.append(self.link.push(b.at[:, cb], rb.at[o - 1], device))
        return copies

    def summed(self, axis, wide, narrow, a, b, ra, rb):
        own = self.place.coord(axis)
        ca = pl.ds(pl.multiple_of(own * wide, 128), wide)
        cb = pl.ds(pl.multiple_of(own * narrow, 128), narrow)
        return (
            a[:, ca] + (ra[0].astype(F32) + ra[1].astype(F32) + ra[2].astype(F32)),
            b[:, cb] + (rb[0].astype(F32) + rb[1].astype(F32) + rb[2].astype(F32)),
        )

    def steps(self):
        place, push = self.place, self.link.push
        a0, b0, a0n, b0n, a1, b1, ra1, rb1, a2, b2, ra2, rb2, ra3, rb3, sq, rsq = self.bufs
        half = RANK // 2
        mine = pl.ds(pl.multiple_of(place.c * half, half), half)
        theirs = pl.ds(pl.multiple_of((1 - place.c) * half, half), half)
        partner = place.partner()

        def arrived(copies):
            for copy in copies:
                copy.wait_recv()

        copies = [push(self.sa.at[theirs], a0, partner), push(self.sb.at[theirs], b0, partner)]
        yield
        arrived(copies)
        a0[...] += self.sa[mine]
        b0[...] += self.sb[mine]
        a0n[...] = a0[...].astype(BF16)
        b0n[...] = b0[...].astype(BF16)
        copies = self.spread("y", 1024, 512, a0n, b0n, ra1, rb1)
        yield
        arrived(copies)
        a1[...], b1[...] = self.summed("y", 1024, 512, a0, b0, ra1, rb1)
        copies = self.spread("z", 256, 128, a1, b1, ra2, rb2)
        yield
        arrived(copies)
        a2[mine], b2[mine] = self.summed("z", 256, 128, a1, b1, ra2, rb2)
        copies = []
        for o in (1, 2, 3):
            device = place.along("x", o)
            copies.append(push(a2.at[mine], ra3.at[o - 1], device))
            copies.append(push(b2.at[mine], rb3.at[o - 1], device))
        yield
        arrived(copies)
        self.link.settle(copies)
        a2[mine] += ra3[0] + ra3[1] + ra3[2]
        b2[mine] += rb3[0] + rb3[1] + rb3[2]
        copies = [push(a2.at[mine], a2.at[mine], partner), push(b2.at[mine], b2.at[mine], partner)]
        yield
        arrived(copies)
        a = a2[...]
        b = b2[...]
        row = lax.broadcasted_iota(jnp.int32, (8, 128), 0)
        sq[0] = jnp.where(row == 0, jnp.sum(a * a), jnp.sum(b * b))
        for i, axis in enumerate("yz"):
            copies = [push(sq.at[i], rsq.at[i, o - 1], place.along(axis, o)) for o in (1, 2, 3)]
            yield
            arrived(copies)
            sq[i + 1] = sq[i] + (rsq[i, 0] + rsq[i, 1] + rsq[i, 2])
        total = sq[2]
        root_a = jnp.sqrt(total[0:1, 0:1] / (RANK * INNER) + CLIP_EPSILON)
        root_b = jnp.sqrt(total[1:2, 0:1] / (RANK * OUTF) + CLIP_EPSILON)
        a = jnp.where(place.ctx >= 4, a2[:, 128:], a2[:, :128]) / jnp.maximum(1.0, root_a)
        b = b2[...] / jnp.maximum(1.0, root_b)
        a = pltpu.roll(a, lax.rem(256 - 32 * place.ctx, 128), 1)
        b = pltpu.roll(b, lax.rem(128 - 16 * place.ctx, 128), 1)
        self.da[...] = a.T[:32, :]
        self.db[...] = b.T[:16, :]
        yield


def decay_tables(dtu_ref, bias_ref, alog_ref, skip_in, cd_ref, rows_ref, tot_ref, skip_ref):
    step = jax.nn.softplus(dtu_ref[...].T + bias_ref[...])
    run = -jnp.exp(alog_ref[...]) * step
    rows = lax.broadcasted_iota(jnp.int32, (Q, H), 0)
    shift = 1
    while shift < Q:
        run = run + jnp.where(rows >= shift, pltpu.roll(run, shift, 0), 0.0)
        shift *= 2
    both = jnp.concatenate([run, step], axis=1)
    cd_ref[...] = both
    turned = both.T
    for h in range(H):
        rows_ref[h] = turned[h : h + 1, :]
    low = low_lanes(8)
    last = both[Q - 1 : Q, :]
    for p in range(H // 2):
        pair = jnp.where(low, last[:, 2 * p : 2 * p + 1], last[:, 2 * p + 1 : 2 * p + 2])
        tot_ref[p // PAIRS, p % PAIRS] = pair
        skip = skip_in[...]
        skip_ref[:, p * 128 : (p + 1) * 128] = jnp.where(
            low[:1], skip[:, 2 * p : 2 * p + 1], skip[:, 2 * p + 1 : 2 * p + 2]
        )


def masked(keep, tile):
    return jnp.where(keep, tile, 0.0)


def pairs_loop(g, width, body, first=0, last=PAIRS):
    def step(i, carry):
        for u in range(width):
            body(g * PAIRS + i * width + u)
        return carry

    lax.fori_loop(first // width, last // width, step, 0)


def forward_group(g, first, last, x, b, c, skip_ref, cd_ref, rows_ref, prod, turned, ssd, s_ref):
    cs = slice(g * N, (g + 1) * N)
    bg = b[:, cs]
    if first == 0:
        turned[...] = bg.astype(F32).T
        ri = lax.broadcasted_iota(jnp.int32, (Q, Q), 0)
        ci = lax.broadcasted_iota(jnp.int32, (Q, Q), 1)
        prod[...] = masked(ri >= ci, dot_t(c[:, cs], bg))
    low = low_lanes(Q)

    def body(p):
        at = lanes_at(p)
        cols = pair_cols(cd_ref, p)
        xp = x[:, at].astype(F32)
        xdt = (xp * pair_lanes(cols, H, low)).astype(BF16)
        tops, lows, states = [], [], []
        for e in (0, 1):
            col = cols[:, e : e + 1]
            row = rows_ref[2 * p + e]
            s00 = (prod[:128, :128] * jnp.exp(jnp.minimum(col[:128] - row[:, :128], 0.0))).astype(BF16)
            s10 = (prod[128:, :128] * jnp.exp(jnp.minimum(col[128:] - row[:, :128], 0.0))).astype(BF16)
            s11 = (prod[128:, 128:] * jnp.exp(jnp.minimum(col[128:] - row[:, 128:], 0.0))).astype(BF16)
            tops.append(dot(s00, xdt[:128]))
            lows.append(dot(jnp.concatenate([s10, s11], axis=1), xdt))
            bw = (turned[...] * jnp.exp(row[:, Q - 1 : Q] - row)).astype(BF16)
            states.append(dot(bw, xdt))
        skip = skip_ref[:, at]
        ssd[:128, at] = jnp.where(low[:128], tops[0], tops[1]) + skip * xp[:128]
        ssd[128:, at] = jnp.where(low[:128], lows[0], lows[1]) + skip * xp[128:]
        s_ref[g, p - g * PAIRS] = jnp.where(low[:N], states[0], states[1]).astype(BF16)

    pairs_loop(g, 2, body, first, last)


ROWS = 64


def rows_loop(body):
    def step(i, carry):
        body(pl.ds(pl.multiple_of(i * ROWS, ROWS), ROWS))
        return carry

    lax.fori_loop(0, Q // ROWS, step, 0)


def silu_of(z, at, gs):
    zf = z[at, gs].astype(F32)
    return 0.5 * zf * (1.0 + jnp.tanh(0.5 * zf))


def norm_group(g, z, c, inc, gain_ref, cd_ref, ssd, stat, normed, down, up_t, down_t, sa):
    gs = slice(g * GW, (g + 1) * GW)
    cg = c[:, g * N : (g + 1) * N]
    low = low_lanes(Q)

    def inter(p):
        at = lanes_at(p)
        cols = pair_cols(cd_ref, p)
        ssd[:, at] += jnp.exp(pair_lanes(cols, 0, low)) * dot(cg, inc[g, p - g * PAIRS])

    pairs_loop(g, 2, inter)
    gain = gain_ref[:, gs]

    def chunk(at):
        gated = ssd[at, gs] * silu_of(z, at, gs)
        rstd = lax.rsqrt(jnp.mean(gated * gated, axis=-1, keepdims=True) + EPS_NORM)
        hat = gated * rstd
        ssd[at, gs] = hat
        stat[g, at, :] = jnp.broadcast_to(rstd, (ROWS, 128))
        normed[at, :] = (hat * gain).astype(BF16)

    rows_loop(chunk)
    sa[:, gs] = SCALE * dot(up_t[...], normed[...])
    part = dot_t(down[:, gs], normed[...])
    if g == 0:
        down_t[...] = part
    else:
        down_t[...] += part


def gradient_group(g, z, c, wbuf, cot, down, up_row, gain_ref, rows_ref, ssd, stat, dn, turned, d, grad):
    gs = slice(g * GW, (g + 1) * GW)

    def column(i, carry):
        at = pl.ds(pl.multiple_of(i * 256, 256), 256)
        full = pl.ds(pl.multiple_of(g * GW + i * 256, 256), 256)
        w = wbuf[:, :, :, :, g, :, at].reshape(OUTF, 256)
        dn[:, at] = dot(cot[...], w) + SCALE * dot(up_row[...], down[:, full])
        return carry

    lax.fori_loop(0, GW // 256, column, 0)
    gain = gain_ref[:, gs]

    def chunk(at):
        hat = ssd[at, gs]
        wg = dn[at, :] * gain
        slope = jnp.mean(hat * wg, axis=-1, keepdims=True)
        d[at, gs] = (stat[g, at, 0:1] * (wg - hat * slope) * silu_of(z, at, gs)).astype(BF16)

    rows_loop(chunk)
    turned[...] = c[:, g * N : (g + 1) * N].astype(F32).T
    low_n = low_lanes(N)

    def body(p):
        dp = d[:, lanes_at(p)]
        halves = []
        for e in (0, 1):
            cw = (turned[...] * jnp.exp(rows_ref[2 * p + e])).astype(BF16)
            halves.append(dot(cw, dp))
        grad[g, p - g * PAIRS] = jnp.where(low_n, halves[0], halves[1]).astype(BF16)

    pairs_loop(g, 2, body)


def backward_group(g, b, c, d, outg, skip_ref, cd_ref, rows_ref, prod, o):
    cs = slice(g * N, (g + 1) * N)
    bg = b[:, cs]
    ri = lax.broadcasted_iota(jnp.int32, (Q, Q), 0)
    ci = lax.broadcasted_iota(jnp.int32, (Q, Q), 1)
    prod[...] = masked(ci >= ri, dot_t(bg, c[:, cs]))
    low = low_lanes(Q)

    def body(p):
        at = lanes_at(p)
        cols = pair_cols(cd_ref, p)
        dp = d[:, at]
        tops, lows = [], []
        for e in (0, 1):
            col = cols[:, e : e + 1]
            row = rows_ref[2 * p + e]
            s00 = (prod[:128, :128] * jnp.exp(jnp.minimum(row[:, :128] - col[:128], 0.0))).astype(BF16)
            s01 = (prod[:128, 128:] * jnp.exp(jnp.minimum(row[:, 128:] - col[:128], 0.0))).astype(BF16)
            s11 = (prod[128:, 128:] * jnp.exp(jnp.minimum(row[:, 128:] - col[128:], 0.0))).astype(BF16)
            tops.append(dot(jnp.concatenate([s00, s01], axis=1), dp))
            lows.append(dot(s11, dp[128:]))
        run = pair_lanes(cols, 0, low)
        cross = jnp.exp(run[Q - 1 : Q] - run) * dot(bg, outg[g, p - g * PAIRS])
        dt = pair_lanes(cols, H, low)
        skip = skip_ref[:, at]
        top = jnp.where(low[:128], tops[0], tops[1]) + cross[:128]
        bottom = jnp.where(low[:128], lows[0], lows[1]) + cross[128:]
        o[:128, at] = (dt[:128] * top + skip * dp[:128].astype(F32)).astype(BF16)
        o[128:, at] = (dt[128:] * bottom + skip * dp[128:].astype(F32)).astype(BF16)

    pairs_loop(g, 2, body)


SLOTS = 340
HALF = RANK // 2
VMEM_SCRATCH = [
    ("wbuf", (4, 4, 4, 2, G, 16, GW), BF16),
    ("x", (Q, INNER), BF16),
    ("z", (Q, INNER), BF16),
    ("b", (Q, G * N), BF16),
    ("c", (Q, G * N), BF16),
    ("cot", (Q, OUTF), BF16),
    ("down", (RANK, INNER), BF16),
    ("up", (RANK, OUTF), BF16),
    ("skip", (1, INNER), F32),
    ("cd", (Q, 128), F32),
    ("rows", (H, 1, Q), F32),
    ("tot", (G, PAIRS, 8, 128), F32),
    ("tots", (8, G, 8, 128), F32),
    ("prod", (Q, Q), F32),
    ("turned", (N, Q), F32),
    ("ssd", (Q, INNER), F32),
    ("stat", (G, Q, 128), F32),
    ("dn", (Q, GW), F32),
    ("normed", (Q, GW), BF16),
    ("d", (Q, INNER), BF16),
    ("o", (Q, INNER), BF16),
    ("up_t", (RANK, Q), BF16),
    ("up_row", (Q, RANK), BF16),
    ("down_t", (RANK, Q), F32),
    ("sa", (RANK, INNER), F32),
    ("sb", (RANK, OUTF), F32),
    ("s_own", (G, PAIRS, N, 128), BF16),
    ("s_got", (8, G, N, 128), BF16),
    ("s_made", (8, G, N, 128), BF16),
    ("s_out", (G, PAIRS, N, 128), BF16),
    ("g_own", (G, PAIRS, N, 128), BF16),
    ("g_got", (8, G, N, 128), BF16),
    ("g_made", (8, G, N, 128), BF16),
    ("g_out", (G, PAIRS, N, 128), BF16),
    ("a0", (HALF, INNER), F32),
    ("b0", (HALF, OUTF), F32),
    ("a0n", (HALF, INNER), BF16),
    ("b0n", (HALF, OUTF), BF16),
    ("a1", (HALF, 1024), F32),
    ("b1", (HALF, 512), F32),
    ("ra1", (3, HALF, 1024), BF16),
    ("rb1", (3, HALF, 512), BF16),
    ("a2", (RANK, 256), F32),
    ("b2", (RANK, 128), F32),
    ("ra2", (3, HALF, 256), F32),
    ("rb2", (3, HALF, 128), F32),
    ("ra3", (3, HALF, 256), F32),
    ("rb3", (3, HALF, 128), F32),
    ("sq", (3, 8, 128), F32),
    ("rsq", (2, 3, 8, 128), F32),
]
SUM_BUFS = (
    "a0", "b0", "a0n", "b0n", "a1", "b1", "ra1", "rb1", "a2", "b2", "ra2", "rb2", "ra3", "rb3", "sq", "rsq",
)
LOADS = ("x", "b", "c", "cot", "up", "z", "down")


def body(*refs):
    names = (
        "dtu", "bias", "alog", "skip_in", "gain", "w", "x", "b", "c", "cot", "up", "z", "down", "o_hbm", "da", "db",
    )
    r = dict(zip([n + "_in" if n in LOADS else n for n in names], refs))
    rest = refs[len(names) :]
    r.update(zip([n for n, _, _ in VMEM_SCRATCH], rest))
    send_sem, recv_sem, load_sem, own_sem, out_sem = rest[len(VMEM_SCRATCH) :]
    place = Place()
    lines = [place.along(axis, step) for axis in "yz" for step in (1, 2, 3)]

    everyone = greet(lines + [{"dp": place.dp, "ctx": place.position(o)} for o in range(1, 8)])
    own = []
    for g in range(G):
        copy = pltpu.make_async_copy(
            r["w"].at[:, pl.ds(g * GW, GW)],
            r["wbuf"].at[place.y, place.z, place.x, place.c, g],
            own_sem.at[g],
        )
        copy.start()
        own.append(copy)
    loads = {}
    for i, name in enumerate(LOADS):
        loads[name] = pltpu.make_async_copy(r[name + "_in"], r[name], load_sem.at[i])
        loads[name].start()
    link = Link(send_sem, recv_sem)
    weight = Weight(place, link, r["wbuf"])
    fwd = Exchange(place, link, r["s_own"], r["tots"], r["s_got"], r["s_made"], r["s_out"], False)
    bwd = Exchange(place, link, r["g_own"], r["tots"], r["g_got"], r["g_made"], r["g_out"], True)
    sums = Sums(place, link, r["sa"], r["sb"], r["da"], r["db"], [r[n] for n in SUM_BUFS]).steps()

    for copy in own:
        copy.wait()
    everyone()
    weight.step()
    decay_tables(
        r["dtu"], r["bias"], r["alog"], r["skip_in"], r["cd"], r["rows"], r["tot"], r["skip"]
    )
    me = place.ctx
    totals = []
    for o in range(1, 8):
        k = place.position(o)
        totals.append(link.push(r["tot"].at[:, k], r["tots"].at[me], {"dp": place.dp, "ctx": k}))
    r["tots"][me] = r["tot"][:, me]
    for name in ("x", "b", "c"):
        loads[name].wait()

    def forward(g):
        for first, last in ((0, PAIRS // 2), (PAIRS // 2, PAIRS)):
            forward_group(
                g, first, last, r["x"], r["b"], r["c"], r["skip"], r["cd"], r["rows"], r["prod"], r["turned"],
                r["ssd"], r["s_own"],
            )
            if last == PAIRS:
                fwd.scatter(g)
            if weight.at < 7:
                weight.step()

    def norm(g):
        fwd.finish(g)
        norm_group(
            g, r["z"], r["c"], r["s_out"], r["gain"], r["cd"], r["ssd"], r["stat"], r["normed"], r["down"],
            r["up_t"], r["down_t"], r["sa"],
        )

    def gradient(g):
        weight.ready(g)
        gradient_group(
            g, r["z"], r["c"], r["wbuf"], r["cot"], r["down"], r["up_row"], r["gain"], r["rows"], r["ssd"],
            r["stat"], r["dn"], r["turned"], r["d"], r["g_own"],
        )
        bwd.scatter(g)

    results = []

    def backward(g):
        bwd.finish(g)
        backward_group(
            g, r["b"], r["c"], r["d"], r["g_out"], r["skip"], r["cd"], r["rows"], r["prod"], r["o"]
        )
        at = pl.ds(g * GW, GW)
        copy = pltpu.make_async_copy(r["o"].at[:, at], r["o_hbm"].at[:, at], out_sem.at[g])
        copy.start()
        results.append(copy)

    forward(0)
    forward(1)
    for copy in totals:
        copy.wait_recv()
    forward(2)
    fwd.combine(0)
    forward(3)
    fwd.combine(1)
    weight.step()
    for name in ("cot", "up", "z", "down"):
        loads[name].wait()
    r["up_t"][...] = dot_t(r["up"][...], r["cot"][...]).astype(BF16)
    r["up_row"][...] = dot_t(r["cot"][...], r["up"][...]).astype(BF16)
    fwd.combine(2)
    norm(0)
    weight.step()
    fwd.combine(3)
    norm(1)
    norm(2)
    weight.step()
    norm(3)
    r["sb"][...] = SCALE * dot(r["down_t"][...].astype(BF16), r["cot"][...])
    next(sums)
    gradient(0)
    weight.step()
    next(sums)
    gradient(1)
    weight.step()
    bwd.combine(0)
    next(sums)
    gradient(2)
    bwd.combine(1)
    next(sums)
    gradient(3)
    bwd.combine(2)
    next(sums)
    backward(0)
    next(sums)
    bwd.combine(3)
    backward(1)
    next(sums)
    backward(2)
    next(sums)
    backward(3)
    for copy in results:
        copy.wait()
    link.drain()


def run_all(dtu, bias, alog, skip, gain, w, x, b, c, cot, up, z, down):
    vmem = pl.BlockSpec(memory_space=pltpu.VMEM)
    hbm = pl.BlockSpec(memory_space=pl.ANY)
    return pl.pallas_call(
        body,
        in_specs=[vmem] * 5 + [hbm] * 8,
        out_specs=[hbm, vmem, vmem],
        out_shape=[
            jax.ShapeDtypeStruct((Q, INNER), BF16),
            jax.ShapeDtypeStruct((32, RANK), F32),
            jax.ShapeDtypeStruct((16, RANK), F32),
        ],
        scratch_shapes=[pltpu.VMEM(shape, dtype) for _, shape, dtype in VMEM_SCRATCH]
        + [
            pltpu.SemaphoreType.DMA((SLOTS,)),
            pltpu.SemaphoreType.DMA((SLOTS,)),
            pltpu.SemaphoreType.DMA((len(LOADS),)),
            pltpu.SemaphoreType.DMA((G,)),
            pltpu.SemaphoreType.DMA((G,)),
        ],
        compiler_params=pltpu.CompilerParams(
            collective_id=1, has_side_effects=True, vmem_limit_bytes=VMEM_LIMIT
        ),
        name="whole_step",
    )(dtu, bias, alog, skip, gain, w, x, b, c, cot, up, z, down)


def on_device(x, z, b, c, dtu, bias, alog, skip, gain, down, up, w, cot):
    dx, da, db = run_all(
        dtu.T,
        bias.reshape(1, H),
        alog.reshape(1, H),
        skip.reshape(1, H),
        gain.reshape(1, INNER),
        w,
        x,
        b,
        c,
        cot,
        up,
        z,
        down,
    )
    return dx, da.T, db.T


def solution(mesh):
    rows = P(("dp", "ctx"), None)
    placed = (rows,) * 5 + (P(),) * 6 + (rows, rows)
    return jax.shard_map(
        on_device,
        mesh=mesh,
        in_specs=placed,
        out_specs=(rows, P(None, ("dp", "ctx")), P(None, ("dp", "ctx"))),
        check_vma=False,
    )
```

time: 576 us -> 116 us (0.20)
  waiting for transfers between devices: 225 us -> 0 us
  local copies, waits for them, and re-layouts: 132 us -> 4.35 us
  other arithmetic: 127 us -> 0 us
  Pallas kernels: 0 us -> 111 us
  matrix products: 49.5 us -> 0 us
  blocking collectives: 20.2 us -> 0 us
  between operations: 15.8 us -> 0.66 us
    psum x1 -> x0, waiting for transfers between devices: 116 us -> none  [on_device(): down_total, up_total = lax.psum((down_portion, up_portion), ('dp', 'ctx'))]
    pallas_call x0 -> x1, Pallas kernels: none -> 111 us  [run_all(): pl.pallas_call(body, in_specs=[vmem] * 5 + [hbm] * 8, out_specs=[hbm, vme...]
    all_gather x3 -> x0, waiting for transfers between devices: 109 us -> none  [the longest x1 67.2 us: entering(): pieces = jax.tree.map(lambda part: lax.all_gather(part, axis), value)]
    dynamic_slice x28 -> x0, local copies, waits for them, and re-layouts: 62.2 us -> none  [the longest x14 32.2 us: lap(): longer = join(running, jax.tree.map(lambda part: part[position], pieces))]
    dot_general x12 -> x0, matrix products: 49.5 us -> none  [the longest x1 8.33 us: on_device(): jnp.einsum('kjhn,khnp->kjhp', b_weighted, outgoing_bf, preferred_element_...]
    select_n x7 -> x0, other arithmetic: 43 us -> none  [lap(): jnp.where(position < mine, new, old)]
    add x7 -> x0, other arithmetic: 32.7 us -> none  [combine(): earlier[1] * later[0][:, None, None] + later[1]]
    convert_element_type x14 -> x0, other arithmetic: 30.6 us -> none  [the longest x1 7.27 us: on_device(): grad_heads.reshape(row_count, INNER_CHANNELS).astype(jnp.bfloat16)]
  transfers between devices with their start and end apart: 4 -> 0, of which waited for: 3 -> 0; matrix products, arithmetic and copies ran while one was open for 27% -> 0% of each run, Pallas kernels for 0% -> 0%
where the time goes in v2:
time: 116 us
  Pallas kernels  111 us (96%)
  local copies, waits for them, and re-layouts  4.35 us (4%)
    pallas_call x1, Pallas kernels, run_all(): pl.pallas_call(body, in_specs=[vmem] * 5 + [hbm] * 8, out_specs=[hbm, vme...  111 us
    unnamed x7, local copies, waits for them, and re-layouts  4.35 us

profile of v2, /device:TPU:0, one launch (start us, length us, event | category | flops | bytes accessed | tf_op | source)
XLA Modules:
  0.0 115.6 jit_solution(17836254187128102285)
XLA Ops:
  0.6 110.6 %whole_step.1 = (bf16[256,4096]{1,0:T(8,128)(2,1)}, f32[32,64]{1,0:T(8,128)}, f32[16,64]{1,0:T(8,128)}) custom-call(f32[64,256]{1,0:T(8,128)} %bitcast.7, f32[1,64]{1,0:T(1,128)} %bitcast.11, f32[1,64]{1,0:T(1,128)} %bitcast.12, f32[1,64]{1,0:T(1,128)} %bitcast.13, f32[1,4096]{1,0:T(1,128)} %bitcast.8, bf16[16,4096]{1,0:T(8,128)(2,1)} %refs_5_.1, ...), custom_call_target="tpu_custom_call" | custom-call | tf_op jit(solution)/shard_map/whole_step/pallas_call | solution.py:748
  111.3 0.0 copy-start
  111.3 0.0 copy-start.1
  111.3 3.1 %copy.19 = bf16[256,4096]{1,0:T(8,128)(2,1)} copy(bf16[256,4096]{1,0:T(8,128)(2,1)} %get-tuple-element.12) | data formatting | bytes 4194304
  114.4 0.0 copy-done
  114.4 0.6 copy.20
  115.0 0.0 copy-done.1
  115.0 0.6 copy.21
Async XLA Ops:
  111.3 3.2 %copy-start = (f32[32,64]{1,0:T(8,128)S(1)}, f32[32,64]{1,0:T(8,128)}, u32[]{:S(2)}) copy-start(f32[32,64]{1,0:T(8,128)} %get-tuple-element.7) | copy-start | bytes 24580
  111.3 3.8 %copy-start.1 = (f32[16,64]{1,0:T(8,128)S(1)}, f32[16,64]{1,0:T(8,128)}, u32[]{:S(2)}) copy-start(f32[16,64]{1,0:T(8,128)} %get-tuple-element.8) | copy-start | bytes 12292

commit v3 on v2

--- a/solution.py
+++ b/solution.py
@@ -22,7 +22,7 @@
 MESH = pl.DeviceIdType.MESH
 F32 = jnp.float32
 BF16 = jnp.bfloat16
-VMEM_LIMIT = 62 * 1024 * 1024
+VMEM_LIMIT = 56 * 1024 * 1024
 
 
 def dot(a, b):
@@ -146,20 +146,19 @@
             copy.wait_recv()
 
 
-PARTS = (
-    (("x", "y", "z"), 0, 3),
-    (("y", "z", "x"), 3, 2),
-    (("x", "z", "y"), 5, 3),
-)
+ORDERS = (("x", "y", "z"), ("y", "z", "x"), ("x", "z", "y"))
+TILES = ((4, 1, 3), (3, 1, 4), (3, 2, 3), (3, 2, 3))
 
 
 class Part:
-    def __init__(self, place, link, buf, order, start, tiles):
+    def __init__(self, place, link, buf, index):
         self.place, self.link, self.buf = place, link, buf
-        self.order, self.start, self.tiles = order, start, tiles
+        self.order = ORDERS[index]
+        self.start = [sum(tiles[:index]) for tiles in TILES]
+        self.tiles = [tiles[index] for tiles in TILES]
         self.near, self.far = {}, {}
 
-    def view(self, stage, step, group=None, groups=None, tiles=None):
+    def view(self, stage, step, g, tiles=None):
         picks = {}
         for i, axis in enumerate(self.order):
             if i < stage:
@@ -168,24 +167,26 @@
                 picks[axis] = lax.rem(self.place.coord(axis) + step, 4)
             else:
                 picks[axis] = self.place.coord(axis)
-        lo, count = (0, self.tiles) if tiles is None else tiles
-        where = groups if group is None else group
-        if where is None:
-            where = slice(None)
+        lo, count = (0, self.tiles[g]) if tiles is None else tiles
         return self.buf.at[
             picks["y"],
             picks["z"],
             picks["x"],
             self.place.c,
-            where,
+            g,
             slice(None),
-            pl.ds((self.start + lo) * 128, count * 128),
+            pl.ds((self.start[g] + lo) * 128, count * 128),
         ]
 
     def push(self, view, device):
         return self.link.push(view, view, device)
 
-    def hop_one(self, stage, g=None):
+    def direct(self, stage, g):
+        axis = self.order[stage]
+        view = self.view(stage, 0, g)
+        self.far[stage, g] = [self.push(view, self.place.along(axis, o)) for o in (1, 3, 2)]
+
+    def hop_one(self, stage, g):
         axis = self.order[stage]
         view = self.view(stage, 0, g)
         self.near[stage, g] = (
@@ -193,27 +194,22 @@
             self.push(view, self.place.along(axis, 3)),
         )
 
-    def cut(self, g):
-        if g is None:
-            return {"groups": slice(0, 2)}, {"groups": slice(2, 4)}
-        lo = (self.tiles + 1 - g % 2) // 2
-        low = {"group": g, "tiles": (0, lo)} if lo else None
-        high = {"group": g, "tiles": (lo, self.tiles - lo)} if lo < self.tiles else None
-        return low, high
-
-    def hop_two(self, stage, g=None):
+    def hop_two(self, stage, g):
         axis = self.order[stage]
-        low, high = self.cut(g)
+        count = self.tiles[g]
+        lo = (count + 1 - g % 2) // 2
         left, right = self.near[stage, g]
         self.far[stage, g] = []
         left.wait_recv()
-        if low is not None:
-            self.far[stage, g].append(self.push(self.view(stage, 3, **low), self.place.along(axis, 1)))
+        if lo:
+            self.far[stage, g].append(self.push(self.view(stage, 3, g, (0, lo)), self.place.along(axis, 1)))
         right.wait_recv()
-        if high is not None:
-            self.far[stage, g].append(self.push(self.view(stage, 1, **high), self.place.along(axis, 3)))
-
-    def arrive(self, stage, g=None):
+        if lo < count:
+            self.far[stage, g].append(
+                self.push(self.view(stage, 1, g, (lo, count - lo)), self.place.along(axis, 3))
+            )
+
+    def arrive(self, stage, g):
         for copy in self.far[stage, g]:
             copy.wait_recv()
 
@@ -223,41 +219,31 @@
 
 class Weight:
     def __init__(self, place, link, buf):
-        self.parts = [Part(place, link, buf, *part) for part in PARTS]
+        self.parts = [Part(place, link, buf, i) for i in range(3)]
         self.shared = {g: [] for g in range(G)}
-        self.plan = (
-            (lambda: self.one(0, None),),
-            (lambda: self.two(0, None),),
-            (lambda: self.one(1, 0, (0, None)), lambda: self.one(1, 1)),
-            (lambda: self.two(1, 0), lambda: self.one(1, 2)),
-            (lambda: self.last(0), lambda: self.two(1, 1), lambda: self.one(1, 3)),
-            (lambda: self.last(1), lambda: self.two(1, 2)),
-            (lambda: self.relay(0), lambda: self.last(2), lambda: self.two(1, 3)),
-            (lambda: self.relay(1), lambda: self.last(3)),
-            (lambda: self.land(0), lambda: self.relay(2)),
-            (lambda: self.land(1), lambda: self.relay(3)),
-            (lambda: self.land(2),),
-            (lambda: self.land(3),),
-        )
-        self.at = 0
-
-    def step(self):
-        for act in self.plan[self.at]:
-            act()
-        self.at += 1
-
-    def one(self, stage, g, after=None):
+
+    def first(self, g):
         for part in self.parts:
-            if after is not None:
-                part.arrive(*after)
-            part.hop_one(stage, g)
-
-    def two(self, stage, g):
+            part.direct(0, g)
+
+    def jump(self, g):
         for part in self.parts:
-            part.hop_two(stage, g)
+            part.arrive(0, g)
+            part.direct(1, g)
+
+    def one(self, g):
+        for part in self.parts:
+            part.arrive(0, g)
+            part.hop_one(1, g)
+
+    def two(self, g):
+        for part in self.parts:
+            part.hop_two(1, g)
 
     def last(self, g):
-        self.one(2, g, (1, g))
+        for part in self.parts:
+            part.arrive(1, g)
+            part.hop_one(2, g)
         for part in self.parts:
             self.shared[g].append(part.share(0, g))
 
@@ -481,8 +467,7 @@
         down_t[...] += part
 
 
-def gradient_group(g, z, c, wbuf, cot, down, up_row, gain_ref, rows_ref, ssd, stat, dn, turned, d, grad):
-    gs = slice(g * GW, (g + 1) * GW)
+def project_group(g, wbuf, cot, down, up_row, dn):
 
     def column(i, carry):
         at = pl.ds(pl.multiple_of(i * 256, 256), 256)
@@ -492,6 +477,10 @@
         return carry
 
     lax.fori_loop(0, GW // 256, column, 0)
+
+
+def gradient_group(g, z, c, gain_ref, rows_ref, ssd, stat, dn, turned, d, grad):
+    gs = slice(g * GW, (g + 1) * GW)
     gain = gain_ref[:, gs]
 
     def chunk(at):
@@ -548,7 +537,7 @@
     pairs_loop(g, 2, body)
 
 
-SLOTS = 340
+SLOTS = 350
 HALF = RANK // 2
 VMEM_SCRATCH = [
     ("wbuf", (4, 4, 4, 2, G, 16, GW), BF16),
@@ -571,7 +560,6 @@
     ("dn", (Q, GW), F32),
     ("normed", (Q, GW), BF16),
     ("d", (Q, INNER), BF16),
-    ("o", (Q, INNER), BF16),
     ("up_t", (RANK, Q), BF16),
     ("up_row", (Q, RANK), BF16),
     ("down_t", (RANK, Q), F32),
@@ -610,12 +598,12 @@
 
 def body(*refs):
     names = (
-        "dtu", "bias", "alog", "skip_in", "gain", "w", "x", "b", "c", "cot", "up", "z", "down", "o_hbm", "da", "db",
+        "dtu", "bias", "alog", "skip_in", "gain", "w", "x", "b", "c", "cot", "up", "z", "down", "o", "da", "db",
     )
     r = dict(zip([n + "_in" if n in LOADS else n for n in names], refs))
     rest = refs[len(names) :]
     r.update(zip([n for n, _, _ in VMEM_SCRATCH], rest))
-    send_sem, recv_sem, load_sem, own_sem, out_sem = rest[len(VMEM_SCRATCH) :]
+    send_sem, recv_sem, load_sem, own_sem = rest[len(VMEM_SCRATCH) :]
     place = Place()
     lines = [place.along(axis, step) for axis in "yz" for step in (1, 2, 3)]
 
@@ -642,7 +630,8 @@
     for copy in own:
         copy.wait()
     everyone()
-    weight.step()
+    for g in range(G):
+        weight.first(g)
     decay_tables(
         r["dtu"], r["bias"], r["alog"], r["skip_in"], r["cd"], r["rows"], r["tot"], r["skip"]
     )
@@ -655,16 +644,26 @@
     for name in ("x", "b", "c"):
         loads[name].wait()
 
-    def forward(g):
-        for first, last in ((0, PAIRS // 2), (PAIRS // 2, PAIRS)):
-            forward_group(
-                g, first, last, r["x"], r["b"], r["c"], r["skip"], r["cd"], r["rows"], r["prod"], r["turned"],
-                r["ssd"], r["s_own"],
-            )
-            if last == PAIRS:
-                fwd.scatter(g)
-            if weight.at < 7:
-                weight.step()
+    def forward(g, half):
+        forward_group(
+            g, half * PAIRS // 2, (half + 1) * PAIRS // 2, r["x"], r["b"], r["c"], r["skip"], r["cd"], r["rows"],
+            r["prod"], r["turned"], r["ssd"], r["s_own"],
+        )
+        if half:
+            fwd.scatter(g)
+
+    def total():
+        for copy in totals:
+            copy.wait_recv()
+
+    def lora():
+        for name in ("cot", "up", "z", "down"):
+            loads[name].wait()
+        r["up_t"][...] = dot_t(r["up"][...], r["cot"][...]).astype(BF16)
+        r["up_row"][...] = dot_t(r["cot"][...], r["up"][...]).astype(BF16)
+
+    def lora_sum():
+        r["sb"][...] = SCALE * dot(r["down_t"][...].astype(BF16), r["cot"][...])
 
     def norm(g):
         fwd.finish(g)
@@ -673,72 +672,85 @@
             r["up_t"], r["down_t"], r["sa"],
         )
 
+    def project(g):
+        weight.ready(g)
+        project_group(g, r["wbuf"], r["cot"], r["down"], r["up_row"], r["dn"])
+
     def gradient(g):
-        weight.ready(g)
         gradient_group(
-            g, r["z"], r["c"], r["wbuf"], r["cot"], r["down"], r["up_row"], r["gain"], r["rows"], r["ssd"],
-            r["stat"], r["dn"], r["turned"], r["d"], r["g_own"],
+            g, r["z"], r["c"], r["gain"], r["rows"], r["ssd"], r["stat"], r["dn"], r["turned"], r["d"], r["g_own"]
         )
         bwd.scatter(g)
 
-    results = []
 
     def backward(g):
         bwd.finish(g)
         backward_group(
             g, r["b"], r["c"], r["d"], r["g_out"], r["skip"], r["cd"], r["rows"], r["prod"], r["o"]
         )
-        at = pl.ds(g * GW, GW)
-        copy = pltpu.make_async_copy(r["o"].at[:, at], r["o_hbm"].at[:, at], out_sem.at[g])
-        copy.start()
-        results.append(copy)
-
-    forward(0)
-    forward(1)
-    for copy in totals:
-        copy.wait_recv()
-    forward(2)
+
+    forward(0, 0)
+    forward(0, 1)
+    forward(1, 0)
+    weight.jump(0)
+    weight.one(1)
+    forward(1, 1)
+    forward(2, 0)
+    forward(2, 1)
+    forward(3, 0)
+    weight.last(0)
+    weight.two(1)
+    weight.one(2)
+    forward(3, 1)
+    total()
     fwd.combine(0)
-    forward(3)
+    lora()
+    weight.last(1)
+    weight.two(2)
+    weight.one(3)
     fwd.combine(1)
-    weight.step()
-    for name in ("cot", "up", "z", "down"):
-        loads[name].wait()
-    r["up_t"][...] = dot_t(r["up"][...], r["cot"][...]).astype(BF16)
-    r["up_row"][...] = dot_t(r["cot"][...], r["up"][...]).astype(BF16)
     fwd.combine(2)
     norm(0)
-    weight.step()
+    weight.relay(0)
+    weight.last(2)
+    weight.two(3)
     fwd.combine(3)
     norm(1)
+    weight.relay(1)
+    weight.last(3)
     norm(2)
-    weight.step()
+    weight.land(0)
     norm(3)
-    r["sb"][...] = SCALE * dot(r["down_t"][...].astype(BF16), r["cot"][...])
+    lora_sum()
     next(sums)
+    project(0)
+    weight.relay(2)
+    weight.land(1)
     gradient(0)
-    weight.step()
+    project(1)
+    weight.relay(3)
     next(sums)
+    weight.land(2)
     gradient(1)
-    weight.step()
     bwd.combine(0)
-    next(sums)
+    project(2)
+    weight.land(3)
     gradient(2)
     bwd.combine(1)
+    project(3)
     next(sums)
     gradient(3)
     bwd.combine(2)
     next(sums)
     backward(0)
+    backward(1)
     next(sums)
     bwd.combine(3)
-    backward(1)
     next(sums)
     backward(2)
     next(sums)
     backward(3)
-    for copy in results:
-        copy.wait()
+    next(sums)
     link.drain()
 
 
@@ -748,9 +760,9 @@
     return pl.pallas_call(
         body,
         in_specs=[vmem] * 5 + [hbm] * 8,
-        out_specs=[hbm, vmem, vmem],
+        out_specs=[vmem, vmem, vmem],
         out_shape=[
-            jax.ShapeDtypeStruct((Q, INNER), BF16),
+            pltpu.VMEM((Q, INNER), BF16),
             jax.ShapeDtypeStruct((32, RANK), F32),
             jax.ShapeDtypeStruct((16, RANK), F32),
         ],
@@ -759,7 +771,6 @@
             pltpu.SemaphoreType.DMA((SLOTS,)),
             pltpu.SemaphoreType.DMA((SLOTS,)),
             pltpu.SemaphoreType.DMA((len(LOADS),)),
-            pltpu.SemaphoreType.DMA((G,)),
             pltpu.SemaphoreType.DMA((G,)),
         ],
         compiler_params=pltpu.CompilerParams(

time: 116 us -> 103 us (0.89)
  Pallas kernels: 111 us -> 98.3 us
  local copies, waits for them, and re-layouts: 4.35 us -> 2.53 us
    pallas_call x1, Pallas kernels: 111 us -> 98.3 us  [run_all(): pl.pallas_call(body, in_specs=[vmem] * 5 + [hbm] * 8, out_specs=[vmem, vm...]
    unnamed x7, local copies, waits for them, and re-layouts: 4.35 us -> 2.53 us
where the time goes in v3:
time: 103 us; the launch traced here: 102 us
  Pallas kernels  98.3 us (95%)
  local copies, waits for them, and re-layouts  2.53 us (2%)
    pallas_call x1, Pallas kernels, run_all(): pl.pallas_call(body, in_specs=[vmem] * 5 + [hbm] * 8, out_specs=[vmem, vm...  98.3 us
    unnamed x7, local copies, waits for them, and re-layouts  2.53 us

profile of v3, /device:TPU:0, one launch (start us, length us, event | category | flops | bytes accessed | tf_op | source)
XLA Modules:
  0.0 101.5 jit_solution(1071681797609428912)
XLA Ops:
  0.6 98.3 %whole_step.1 = (bf16[256,4096]{1,0:T(8,128)(2,1)S(1)}, f32[32,64]{1,0:T(8,128)}, f32[16,64]{1,0:T(8,128)}) custom-call(f32[64,256]{1,0:T(8,128)} %bitcast.7, f32[1,64]{1,0:T(1,128)} %bitcast.11, f32[1,64]{1,0:T(1,128)} %bitcast.12, f32[1,64]{1,0:T(1,128)} %bitcast.13, f32[1,4096]{1,0:T(1,128)} %bitcast.8, bf16[16,4096]{1,0:T(8,128)(2,1)} %refs_5_.1, ...), custom_call_target="tpu_custom_call" | custom-call | tf_op jit(solution)/shard_map/whole_step/pallas_call | solution.py:760
  99.0 0.0 copy-start
  99.0 0.0 copy-start.1
  99.0 1.3 %copy.19 = bf16[256,4096]{1,0:T(8,128)(2,1)} copy(bf16[256,4096]{1,0:T(8,128)(2,1)S(1)} %get-tuple-element.9) | data formatting | bytes 4194304
  100.3 0.0 copy-done
  100.3 0.6 copy.20
  100.9 0.0 copy-done.1
  100.9 0.6 copy.21
Async XLA Ops:
  99.0 1.3 %copy-start = (f32[32,64]{1,0:T(8,128)S(1)}, f32[32,64]{1,0:T(8,128)}, u32[]{:S(2)}) copy-start(f32[32,64]{1,0:T(8,128)} %get-tuple-element.7) | copy-start | bytes 24580
  99.0 1.9 %copy-start.1 = (f32[16,64]{1,0:T(8,128)S(1)}, f32[16,64]{1,0:T(8,128)}, u32[]{:S(2)}) copy-start(f32[16,64]{1,0:T(8,128)} %get-tuple-element.8) | copy-start | bytes 12292

commit v4 on v3

--- a/solution.py
+++ b/solution.py
@@ -694,31 +694,31 @@
     forward(1, 0)
     weight.jump(0)
     weight.one(1)
+    weight.one(2)
+    weight.one(3)
     forward(1, 1)
     forward(2, 0)
     forward(2, 1)
-    forward(3, 0)
-    weight.last(0)
-    weight.two(1)
-    weight.one(2)
-    forward(3, 1)
     total()
     fwd.combine(0)
+    forward(3, 0)
+    forward(3, 1)
+    weight.two(1)
+    weight.last(0)
     lora()
+    weight.two(2)
+    weight.two(3)
+    fwd.combine(1)
     weight.last(1)
-    weight.two(2)
-    weight.one(3)
-    fwd.combine(1)
     fwd.combine(2)
     norm(0)
     weight.relay(0)
     weight.last(2)
-    weight.two(3)
     fwd.combine(3)
     norm(1)
+    norm(2)
     weight.relay(1)
     weight.last(3)
-    norm(2)
     weight.land(0)
     norm(3)
     lora_sum()

time: 103 us -> 99.3 us (0.964)
  Pallas kernels: 98.3 us -> 95.1 us
    pallas_call x1, Pallas kernels: 98.3 us -> 95.1 us  [run_all(): pl.pallas_call(body, in_specs=[vmem] * 5 + [hbm] * 8, out_specs=[vmem, vm...]
where the time goes in v4:
time: 99.3 us; the launch traced here: 98.3 us
  Pallas kernels  95.1 us (96%)
  local copies, waits for them, and re-layouts  2.53 us (3%)
    pallas_call x1, Pallas kernels, run_all(): pl.pallas_call(body, in_specs=[vmem] * 5 + [hbm] * 8, out_specs=[vmem, vm...  95.1 us
    unnamed x7, local copies, waits for them, and re-layouts  2.53 us

profile of v4, /device:TPU:0, one launch (start us, length us, event | category | flops | bytes accessed | tf_op | source)
XLA Modules:
  0.0 98.3 jit_solution(10777258759176623531)
XLA Ops:
  0.6 95.1 %whole_step.1 = (bf16[256,4096]{1,0:T(8,128)(2,1)S(1)}, f32[32,64]{1,0:T(8,128)}, f32[16,64]{1,0:T(8,128)}) custom-call(f32[64,256]{1,0:T(8,128)} %bitcast.7, f32[1,64]{1,0:T(1,128)} %bitcast.11, f32[1,64]{1,0:T(1,128)} %bitcast.12, f32[1,64]{1,0:T(1,128)} %bitcast.13, f32[1,4096]{1,0:T(1,128)} %bitcast.8, bf16[16,4096]{1,0:T(8,128)(2,1)} %refs_5_.1, ...), custom_call_target="tpu_custom_call" | custom-call | tf_op jit(solution)/shard_map/whole_step/pallas_call | solution.py:760
  95.7 0.0 copy-start
  95.8 0.0 copy-start.1
  95.8 1.3 %copy.19 = bf16[256,4096]{1,0:T(8,128)(2,1)} copy(bf16[256,4096]{1,0:T(8,128)(2,1)S(1)} %get-tuple-element.9) | data formatting | bytes 4194304
  97.1 0.0 copy-done
  97.1 0.6 copy.20
  97.7 0.0 copy-done.1
  97.7 0.6 copy.21
Async XLA Ops:
  95.7 1.3 %copy-start = (f32[32,64]{1,0:T(8,128)S(1)}, f32[32,64]{1,0:T(8,128)}, u32[]{:S(2)}) copy-start(f32[32,64]{1,0:T(8,128)} %get-tuple-element.7) | copy-start | bytes 24580
  95.8 1.9 %copy-start.1 = (f32[16,64]{1,0:T(8,128)S(1)}, f32[16,64]{1,0:T(8,128)}, u32[]{:S(2)}) copy-start(f32[16,64]{1,0:T(8,128)} %get-tuple-element.8) | copy-start | bytes 12292

commit v5 on v4

--- a/solution.py
+++ b/solution.py
@@ -740,14 +740,14 @@
     project(3)
     next(sums)
     gradient(3)
+    next(sums)
     bwd.combine(2)
-    next(sums)
     backward(0)
     backward(1)
-    next(sums)
     bwd.combine(3)
     next(sums)
     backward(2)
+    next(sums)
     next(sums)
     backward(3)
     next(sums)

time: 99.3 us -> 102 us (1.027)
  Pallas kernels: 95.1 us -> 97.9 us
    pallas_call x1, Pallas kernels: 95.1 us -> 97.9 us  [run_all(): pl.pallas_call(body, in_specs=[vmem] * 5 + [hbm] * 8, out_specs=[vmem, vm...]
where the time goes in v5:
time: 102 us; the launch traced here: 101 us
  Pallas kernels  97.9 us (96%)
  local copies, waits for them, and re-layouts  2.53 us (2%)
    pallas_call x1, Pallas kernels, run_all(): pl.pallas_call(body, in_specs=[vmem] * 5 + [hbm] * 8, out_specs=[vmem, vm...  97.9 us
    unnamed x7, local copies, waits for them, and re-layouts  2.53 us

profile of v5, /device:TPU:0, one launch (start us, length us, event | category | flops | bytes accessed | tf_op | source)
XLA Modules:
  0.0 101.1 jit_solution(17312262448536355561)
XLA Ops:
  0.6 97.9 %whole_step.1 = (bf16[256,4096]{1,0:T(8,128)(2,1)S(1)}, f32[32,64]{1,0:T(8,128)}, f32[16,64]{1,0:T(8,128)}) custom-call(f32[64,256]{1,0:T(8,128)} %bitcast.7, f32[1,64]{1,0:T(1,128)} %bitcast.11, f32[1,64]{1,0:T(1,128)} %bitcast.12, f32[1,64]{1,0:T(1,128)} %bitcast.13, f32[1,4096]{1,0:T(1,128)} %bitcast.8, bf16[16,4096]{1,0:T(8,128)(2,1)} %refs_5_.1, ...), custom_call_target="tpu_custom_call" | custom-call | tf_op jit(solution)/shard_map/whole_step/pallas_call | solution.py:760
  98.5 0.0 copy-start
  98.5 0.0 copy-start.1
  98.5 1.3 %copy.19 = bf16[256,4096]{1,0:T(8,128)(2,1)} copy(bf16[256,4096]{1,0:T(8,128)(2,1)S(1)} %get-tuple-element.9) | data formatting | bytes 4194304
  99.9 0.0 copy-done
  99.9 0.6 copy.20
  100.5 0.0 copy-done.1
  100.5 0.6 copy.21
Async XLA Ops:
  98.5 1.3 %copy-start = (f32[32,64]{1,0:T(8,128)S(1)}, f32[32,64]{1,0:T(8,128)}, u32[]{:S(2)}) copy-start(f32[32,64]{1,0:T(8,128)} %get-tuple-element.7) | copy-start | bytes 24580
  98.5 1.9 %copy-start.1 = (f32[16,64]{1,0:T(8,128)S(1)}, f32[16,64]{1,0:T(8,128)}, u32[]{:S(2)}) copy-start(f32[16,64]{1,0:T(8,128)} %get-tuple-element.8) | copy-start | bytes 12292
